TPU v7x, 512 devices: a whole 4x8x8 slice. The times are simulated.
512 devices in a mesh: pair: 256 (over z, y, x), aux: 2 (over core).
Axes of the slice: x: 4, y: 8, z: 8, core: 2. Of those that a mesh axis runs over, the one named last changes fastest.
Arguments:
- amplitudes: bfloat16 [256, 256, 256], P('pair'), may hold values from -6 to 6
- ranks: int32 [256], P('pair'), may hold values from 64 to 256
- neighbours: int32 [256, 16], P('pair', 'aux'), may hold values from 0 to 255, as said below
- intersections: bfloat16 [256, 16, 256, 256], P('pair', 'aux'), may hold values from -0.375 to 0.375
- couplings: float32 [256, 16], P('pair', 'aux'), may hold values from -1 to 1
- energies: float32 [256, 256], P('pair'), may hold values from 0.5 to 4
- factors: bfloat16 [256, 2, 5120, 256], P('pair', None, 'aux'), may hold values from -1.75 to 1.75
Outputs:
- residual: float32 [256, 256, 256], P('pair', 'aux')
- updated: float32 [256, 256, 256], P('pair', 'aux')
Inputs may be any that keep to these rules, and one draw needn't show every extreme that they name: `neighbours`: the 16 coupled pairs of pair p are distinct and lie among the pairs p - 8 to p + 8, counted modulo 256.
All inputs are finite; a program needn't handle non-finite values.
Results may differ from a plain program's by a relative error of at most 0.0022.
Values may be sent and summed in bfloat16 or wider, within the bound.
A program may use at most 64 MiB of HBM per device.

v0:
```python
import jax
import jax.numpy as jnp
from jax import lax
from jax.sharding import PartitionSpec as P

WIN = 8


def shifted(value, axis, steps):
    count = lax.axis_size(axis)
    pairs = [(source, (source + steps) % count) for source in range(count)]
    return lax.ppermute(value, axis, pairs)


def shards(amplitudes, ranks, neighbours, intersections, couplings, energies, factors):
    pair_dev = amplitudes.shape[0]
    pno_width = amplitudes.shape[1]
    aux_count = lax.axis_size("aux")
    pair_count = lax.axis_size("pair")
    row_span = pno_width // aux_count
    aux_index = lax.axis_index("aux")
    first_row = aux_index * row_span
    reach = (WIN + pair_dev - 1) // pair_dev
    positions = jnp.arange(pno_width)
    live_rows = positions[None, :] < ranks[:, None]
    square_mask = live_rows[:, :, None] & live_rows[:, None, :]
    masked = jnp.where(square_mask, amplitudes, jnp.zeros((), jnp.bfloat16))
    blocks = []
    for step in range(-reach, reach + 1):
        if step == 0:
            blocks.append(masked)
        else:
            blocks.append(shifted(masked, "pair", -step))
    extended = jnp.concatenate(blocks, axis=0)
    offset = lax.axis_index("pair") * pair_dev - reach * pair_dev
    nearby = (neighbours - offset) % (pair_dev * pair_count)
    partial_sum = jnp.einsum(
        "pqa,pqb->pab", factors[:, 0], factors[:, 1], preferred_element_type=jnp.float32
    )
    for column in range(neighbours.shape[1]):
        picked = extended[nearby[:, column]]
        intersection_now = intersections[:, column]
        half_product = jnp.einsum(
            "pac,pcd->pad", intersection_now, picked, preferred_element_type=jnp.float32
        ).astype(jnp.bfloat16)
        projected = jnp.einsum(
            "pad,pbd->pab", half_product, intersection_now, preferred_element_type=jnp.float32
        )
        partial_sum = partial_sum + couplings[:, column][:, None, None] * projected
    summed = lax.psum_scatter(partial_sum, "aux", scatter_dimension=1, tiled=True)
    row_energy = lax.dynamic_slice_in_dim(energies, first_row, row_span, 1)
    denominator = row_energy[:, :, None] + energies[:, None, :]
    row_amp = lax.dynamic_slice_in_dim(masked, first_row, row_span, 1).astype(jnp.float32)
    row_mask = lax.dynamic_slice_in_dim(square_mask, first_row, row_span, 1)
    residual = jnp.where(row_mask, summed + denominator * row_amp, jnp.zeros((), jnp.float32))
    return (residual, row_amp - residual / denominator)


def solution(mesh):
    return jax.shard_map(
        shards,
        mesh=mesh,
        in_specs=(
            P("pair", None, None),
            P("pair"),
            P("pair", "aux"),
            P("pair", "aux", None, None),
            P("pair", "aux"),
            P("pair", None),
            P("pair", None, "aux", None),
        ),
        out_specs=(P("pair", "aux", None), P("pair", "aux", None)),
        check_vma=False,
    )
```

profile of v0, /device:TPU:1, one launch (start us, length us, event | category | flops | bytes accessed | tf_op | source)
XLA Modules:
  0.0 154.9 jit_solution(3764993132467802389)
XLA Ops:
  7.9 1.0 broadcast_select_fusion
  8.9 5.0 %collective-permute-start = (bf16[1,256,256]{2,1,0:T(8,128)(2,1)S(1)}, bf16[1,256,256]{2,1,0:T(8,128)(2,1)S(1)}, u32[]{:S(2)}, u32[]{:S(2)}) collective-permute-start(bf16[1,256,256]{2,1,0:T(8,128)(2,1)S(1)} %broadcast_select_fusion), channel_id=1, source_target_pairs={{0,16},{2,18},{4,20},{6,22},{8,24},{10,26},{12,28},{14,30},{16,32}... | collective-permute-start | bytes 393224 | tf_op jit(solution)/shard_map/ppermute | solution.py:12
  14.0 5.4 %collective-permute-start.1 = (bf16[1,256,256]{2,1,0:T(8,128)(2,1)S(1)}, bf16[1,256,256]{2,1,0:T(8,128)(2,1)}, u32[]{:S(2)}, u32[]{:S(2)}) collective-permute-start(bf16[1,256,256]{2,1,0:T(8,128)(2,1)S(1)} %broadcast_select_fusion), channel_id=1, source_target_pairs={{0,14},{2,16},{4,18},{6,20},{8,22},{10,24},{12,26},{14,28},{16,30}... | collective-permute-start | bytes 393224 | tf_op jit(solution)/shard_map/ppermute | solution.py:12
  19.4 4.8 %collective-permute-start.2 = (bf16[1,256,256]{2,1,0:T(8,128)(2,1)S(1)}, bf16[1,256,256]{2,1,0:T(8,128)(2,1)}, u32[]{:S(2)}, u32[]{:S(2)}) collective-permute-start(bf16[1,256,256]{2,1,0:T(8,128)(2,1)S(1)} %broadcast_select_fusion), channel_id=1, source_target_pairs={{0,12},{2,14},{4,16},{6,18},{8,20},{10,22},{12,24},{14,26},{16,28}... | collective-permute-start | bytes 393224 | tf_op jit(solution)/shard_map/ppermute | solution.py:12
  24.2 2.6 %collective-permute-start.3 = (bf16[1,256,256]{2,1,0:T(8,128)(2,1)S(1)}, bf16[1,256,256]{2,1,0:T(8,128)(2,1)}, u32[]{:S(2)}, u32[]{:S(2)}) collective-permute-start(bf16[1,256,256]{2,1,0:T(8,128)(2,1)S(1)} %broadcast_select_fusion), channel_id=1, source_target_pairs={{0,10},{2,12},{4,14},{6,16},{8,18},{10,20},{12,22},{14,24},{16,26}... | collective-permute-start | bytes 393224 | tf_op jit(solution)/shard_map/ppermute | solution.py:12
  26.8 2.3 %collective-permute-start.4 = (bf16[1,256,256]{2,1,0:T(8,128)(2,1)S(1)}, bf16[1,256,256]{2,1,0:T(8,128)(2,1)}, u32[]{:S(2)}, u32[]{:S(2)}) collective-permute-start(bf16[1,256,256]{2,1,0:T(8,128)(2,1)S(1)} %broadcast_select_fusion), channel_id=1, source_target_pairs={{0,8},{2,10},{4,12},{6,14},{8,16},{10,18},{12,20},{14,22},{16,24},... | collective-permute-start | bytes 393224 | tf_op jit(solution)/shard_map/ppermute | solution.py:12
  30.5 1.6 %fusion.103 = (f32[1,1]{1,0:T(1,128)}, f32[1,1]{1,0:T(1,128)}, f32[1,1]{1,0:T(1,128)}, f32[1,1]{1,0:T(1,128)}, f32[1,1]{1,0:T(1,128)}, /*index=5*/f32[1,1]{1,0:T(1,128)}, f32[1,1]{1,0:T(1,128)}, f32[1,1]{1,0:T(1,128)}) fusion(f32[1,8]{1,0:T(1,128)} %param.11), kind=kLoop, calls=%fused_computation.101 | loop fusion | bytes 64 | tf_op jit(solution)/shard_map/slice | solution.py:49
  48.4 5.0 %collective-permute-start.5 = (bf16[1,256,256]{2,1,0:T(8,128)(2,1)S(1)}, bf16[1,256,256]{2,1,0:T(8,128)(2,1)S(1)}, u32[]{:S(2)}, u32[]{:S(2)}) collective-permute-start(bf16[1,256,256]{2,1,0:T(8,128)(2,1)S(1)} %broadcast_select_fusion), channel_id=1, source_target_pairs={{0,6},{2,8},{4,10},{6,12},{8,14},{10,16},{12,18},{14,20},{16,22},{... | collective-permute-start | bytes 393224 | tf_op jit(solution)/shard_map/ppermute | solution.py:12
  53.4 0.9 constant_dynamic-update-slice_fusion.16
  54.3 3.1 %collective-permute-start.6 = (bf16[1,256,256]{2,1,0:T(8,128)(2,1)S(1)}, bf16[1,256,256]{2,1,0:T(8,128)(2,1)S(1)}, u32[]{:S(2)}, u32[]{:S(2)}) collective-permute-start(bf16[1,256,256]{2,1,0:T(8,128)(2,1)S(1)} %broadcast_select_fusion), channel_id=1, source_target_pairs={{0,4},{2,6},{4,8},{6,10},{8,12},{10,14},{12,16},{14,18},{16,20},{1... | collective-permute-start | bytes 393224 | tf_op jit(solution)/shard_map/ppermute | solution.py:12
  57.5 0.9 constant_dynamic-update-slice_fusion.15
  58.4 1.9 %collective-permute-start.7 = (bf16[1,256,256]{2,1,0:T(8,128)(2,1)S(1)}, bf16[1,256,256]{2,1,0:T(8,128)(2,1)S(1)}, u32[]{:S(2)}, u32[]{:S(2)}) collective-permute-start(bf16[1,256,256]{2,1,0:T(8,128)(2,1)S(1)} %broadcast_select_fusion), channel_id=1, source_target_pairs={{0,2},{2,4},{4,6},{6,8},{8,10},{10,12},{12,14},{14,16},{16,18},{18... | collective-permute-start | bytes 393224 | tf_op jit(solution)/shard_map/ppermute | solution.py:12
  61.3 8.8 %collective-permute-start.8 = (bf16[1,256,256]{2,1,0:T(8,128)(2,1)S(1)}, bf16[1,256,256]{2,1,0:T(8,128)(2,1)S(1)}, u32[]{:S(2)}, u32[]{:S(2)}) collective-permute-start(bf16[1,256,256]{2,1,0:T(8,128)(2,1)S(1)} %broadcast_select_fusion), channel_id=1, source_target_pairs={{0,510},{2,0},{4,2},{6,4},{8,6},{10,8},{12,10},{14,12},{16,14},{18... | collective-permute-start | bytes 393224 | tf_op jit(solution)/shard_map/ppermute | solution.py:12
  71.0 2.4 %collective-permute-start.9 = (bf16[1,256,256]{2,1,0:T(8,128)(2,1)S(1)}, bf16[1,256,256]{2,1,0:T(8,128)(2,1)S(1)}, u32[]{:S(2)}, u32[]{:S(2)}) collective-permute-start(bf16[1,256,256]{2,1,0:T(8,128)(2,1)S(1)} %broadcast_select_fusion), channel_id=1, source_target_pairs={{0,508},{2,510},{4,0},{6,2},{8,4},{10,6},{12,8},{14,10},{16,12},{1... | collective-permute-start | bytes 393224 | tf_op jit(solution)/shard_map/ppermute | solution.py:12
  74.4 1.9 %collective-permute-start.10 = (bf16[1,256,256]{2,1,0:T(8,128)(2,1)S(1)}, bf16[1,256,256]{2,1,0:T(8,128)(2,1)S(1)}, u32[]{:S(2)}, u32[]{:S(2)}) collective-permute-start(bf16[1,256,256]{2,1,0:T(8,128)(2,1)S(1)} %broadcast_select_fusion), channel_id=1, source_target_pairs={{0,506},{2,508},{4,510},{6,0},{8,2},{10,4},{12,6},{14,8},{16,10},{... | collective-permute-start | bytes 393224 | tf_op jit(solution)/shard_map/ppermute | solution.py:12
  76.3 2.9 %collective-permute-start.11 = (bf16[1,256,256]{2,1,0:T(8,128)(2,1)S(1)}, bf16[1,256,256]{2,1,0:T(8,128)(2,1)S(1)}, u32[]{:S(2)}, u32[]{:S(2)}) collective-permute-start(bf16[1,256,256]{2,1,0:T(8,128)(2,1)S(1)} %broadcast_select_fusion), channel_id=1, source_target_pairs={{0,504},{2,506},{4,508},{6,510},{8,0},{10,2},{12,4},{14,6},{16,8},... | collective-permute-start | bytes 393224 | tf_op jit(solution)/shard_map/ppermute | solution.py:12
  79.3 5.3 %collective-permute-start.12 = (bf16[1,256,256]{2,1,0:T(8,128)(2,1)S(1)}, bf16[1,256,256]{2,1,0:T(8,128)(2,1)S(1)}, u32[]{:S(2)}, u32[]{:S(2)}) collective-permute-start(bf16[1,256,256]{2,1,0:T(8,128)(2,1)S(1)} %broadcast_select_fusion), channel_id=1, source_target_pairs={{0,502},{2,504},{4,506},{6,508},{8,510},{10,0},{12,2},{14,4},{16,6... | collective-permute-start | bytes 393224 | tf_op jit(solution)/shard_map/ppermute | solution.py:12
  84.7 6.2 %collective-permute-start.13 = (bf16[1,256,256]{2,1,0:T(8,128)(2,1)S(1)}, bf16[1,256,256]{2,1,0:T(8,128)(2,1)S(1)}, u32[]{:S(2)}, u32[]{:S(2)}) collective-permute-start(bf16[1,256,256]{2,1,0:T(8,128)(2,1)S(1)} %broadcast_select_fusion), channel_id=1, source_target_pairs={{0,500},{2,502},{4,504},{6,506},{8,508},{10,510},{12,0},{14,2},{16... | collective-permute-start | bytes 393224 | tf_op jit(solution)/shard_map/ppermute | solution.py:12
  91.0 3.4 %collective-permute-start.14 = (bf16[1,256,256]{2,1,0:T(8,128)(2,1)S(1)}, bf16[1,256,256]{2,1,0:T(8,128)(2,1)S(1)}, u32[]{:S(2)}, u32[]{:S(2)}) collective-permute-start(bf16[1,256,256]{2,1,0:T(8,128)(2,1)S(1)} %broadcast_select_fusion), channel_id=1, source_target_pairs={{0,498},{2,500},{4,502},{6,504},{8,506},{10,508},{12,510},{14,0},{... | collective-permute-start | bytes 393224 | tf_op jit(solution)/shard_map/ppermute | solution.py:12
  94.4 6.4 %collective-permute-start.15 = (bf16[1,256,256]{2,1,0:T(8,128)(2,1)S(1)}, bf16[1,256,256]{2,1,0:T(8,128)(2,1)S(1)}, u32[]{:S(2)}, u32[]{:S(2)}) collective-permute-start(bf16[1,256,256]{2,1,0:T(8,128)(2,1)S(1)} %broadcast_select_fusion), channel_id=1, source_target_pairs={{0,496},{2,498},{4,500},{6,502},{8,504},{10,506},{12,508},{14,510}... | collective-permute-start | bytes 393224 | tf_op jit(solution)/shard_map/ppermute | solution.py:12
  101.1 8.4 %collective-permute-done.15 = bf16[1,256,256]{2,1,0:T(8,128)(2,1)S(1)} collective-permute-done((bf16[1,256,256]{2,1,0:T(8,128)(2,1)S(1)}, bf16[1,256,256]{2,1,0:T(8,128)(2,1)S(1)}, u32[]{:S(2)}, u32[]{:S(2)}) %collective-permute-start.15) | collective-permute-done | bytes 131104 | tf_op jit(solution)/shard_map/ppermute | solution.py:12
  109.5 1.2 convolution_multiply_fusion.7
  110.7 3.0 %fusion.5 = f32[256,256]{1,0:T(8,128)} fusion(f32[256,256]{1,0:T(8,128)S(1)} %convolution_multiply_fusion.7, bf16[1,2,2560,256]{3,2,1,0:T(8,128)(2,1)} %param.13), kind=kOutput, calls=%fused_computation.5 | convolution fusion | flops 335609856 | bytes 3145728 | tf_op jit(solution)/shard_map/pqa,pqb->pab/dot_general | solution.py:37
  113.7 2.0 %fusion.17 = f32[256,256]{1,0:T(8,128)S(1)} fusion(f32[256,256]{1,0:T(8,128)} %fusion.5, bf16[17,256,256]{2,1,0:T(8,128)(2,1)S(1)} %constant_dynamic-update-slice_fusion, s32[]{:T(128)} %bitcast.10, bf16[1,8,256,256]{3,2,1,0:T(8,128)(2,1)S(1)} %copy-done, f32[]{:T(128)} %bitcast.8), kind=kOutput, calls=%fused_computation.20 | convolution fusion | flops 67305472 | bytes 917512 | tf_op jit(solution)/shard_map/pad,pbd->pab/dot_general | solution.py:46
  115.7 2.0 %fusion.16 = f32[256,256]{1,0:T(8,128)S(1)} fusion(f32[256,256]{1,0:T(8,128)S(1)} %fusion.17, bf16[17,256,256]{2,1,0:T(8,128)(2,1)} %copy-done.1, s32[]{:T(128)} %bitcast.15, bf16[1,8,256,256]{3,2,1,0:T(8,128)(2,1)S(1)} %copy-done, f32[]{:T(128)} %bitcast.13), kind=kOutput, calls=%fused_computation.18 | convolution fusion | flops 67305472 | bytes 918528 | tf_op jit(solution)/shard_map/pad,pbd->pab/dot_general | solution.py:46
  117.7 2.0 %fusion.15 = f32[256,256]{1,0:T(8,128)S(1)} fusion(f32[256,256]{1,0:T(8,128)S(1)} %fusion.16, bf16[17,256,256]{2,1,0:T(8,128)(2,1)} %copy-done.1, s32[]{:T(128)} %bitcast.20, bf16[1,8,256,256]{3,2,1,0:T(8,128)(2,1)S(1)} %copy-done, f32[]{:T(128)} %bitcast.18), kind=kOutput, calls=%fused_computation.16 | convolution fusion | flops 67305472 | bytes 918528 | tf_op jit(solution)/shard_map/pad,pbd->pab/dot_general | solution.py:46
  119.8 2.0 %fusion.14 = f32[256,256]{1,0:T(8,128)S(1)} fusion(f32[256,256]{1,0:T(8,128)S(1)} %fusion.15, bf16[17,256,256]{2,1,0:T(8,128)(2,1)} %copy-done.1, s32[]{:T(128)} %bitcast.25, bf16[1,8,256,256]{3,2,1,0:T(8,128)(2,1)S(1)} %copy-done, f32[]{:T(128)} %bitcast.23), kind=kOutput, calls=%fused_computation.14 | convolution fusion | flops 67305472 | bytes 918528 | tf_op jit(solution)/shard_map/pad,pbd->pab/dot_general | solution.py:46
  121.7 2.0 %fusion.13 = f32[256,256]{1,0:T(8,128)S(1)} fusion(f32[256,256]{1,0:T(8,128)S(1)} %fusion.14, bf16[17,256,256]{2,1,0:T(8,128)(2,1)} %copy-done.1, s32[]{:T(128)} %bitcast.30, bf16[1,8,256,256]{3,2,1,0:T(8,128)(2,1)S(1)} %copy-done, f32[]{:T(128)} %bitcast.28), kind=kOutput, calls=%fused_computation.12 | convolution fusion | flops 67305472 | bytes 918528 | tf_op jit(solution)/shard_map/pad,pbd->pab/dot_general | solution.py:46
  123.7 1.9 %fusion.12 = f32[256,256]{1,0:T(8,128)S(1)} fusion(f32[256,256]{1,0:T(8,128)S(1)} %fusion.13, bf16[17,256,256]{2,1,0:T(8,128)(2,1)} %copy-done.1, s32[]{:T(128)} %bitcast.35, bf16[1,8,256,256]{3,2,1,0:T(8,128)(2,1)S(1)} %copy-done, f32[]{:T(128)} %bitcast.33), kind=kOutput, calls=%fused_computation.10 | convolution fusion | flops 67305472 | bytes 918528 | tf_op jit(solution)/shard_map/pad,pbd->pab/dot_general | solution.py:46
  125.7 2.7 %fusion.11 = f32[1,256,256]{2,1,0:T(8,128)} fusion(f32[256,256]{1,0:T(8,128)S(1)} %fusion.12, bf16[17,256,256]{2,1,0:T(8,128)(2,1)} %copy-done.1, s32[]{:T(128)} %bitcast.40, bf16[1,8,256,256]{3,2,1,0:T(8,128)(2,1)S(1)} %copy-done, f32[]{:T(128)} %bitcast.38), kind=kOutput, calls=%fused_computation.8 | convolution fusion | flops 67305472 | bytes 918528 | tf_op jit(solution)/shard_map/pad,pbd->pab/dot_general | solution.py:46
  128.6 17.7 %reduce-scatter.2.cloned.1.call-done = f32[1,128,256]{2,1,0:T(8,128)} async-done(((f32[1,256,256]{2,1,0:T(8,128)}), f32[1,128,256]{2,1,0:T(8,128)}) %reduce-scatter.2.cloned.1.call-update) | async-done | bytes 131088 | tf_op jit(solution)/shard_map/reduce_scatter | solution.py:50
  146.3 1.7 %convert_subtract_fusion = (f32[1,128,256]{2,1,0:T(8,128)}, f32[1,128,256]{2,1,0:T(8,128)}) fusion(f32[256]{0:T(256)S(1)} %bitcast.105, f32[128]{0:T(128)S(1)} %fusion.101, bf16[1,256,256]{2,1,0:T(8,128)(2,1)S(1)} %copy-done.4, s32[]{:T(128)S(6)} %select_n.44, f32[1,128,256]{2,1,0:T(8,128)} %reduce-scatter.2.cloned.1.call-done, ...), kind=kLoop, calls=%fused_computation.32 | loop fusion | flops 229376 | bytes 493060 | tf_op jit(solution)/shard_map/sub | solution.py:56
  (51 shorter events, 5.4 us)
Async XLA Ops:
  7.2 77.4 %copy-start.2 = (bf16[1,256,256]{2,1,0:T(8,128)(2,1)S(1)}, bf16[1,256,256]{2,1,0:T(8,128)(2,1)}, u32[]{:S(2)}) copy-start(bf16[1,256,256]{2,1,0:T(8,128)(2,1)} %param.7) | copy-start | bytes 393220
  7.2 139.1 %reduce-scatter.2.cloned.1.call-start = ((), (), s32[]{:S(2)}) async-start(), calls=%async_computation.1 | async-start | bytes 393216 | tf_op jit(solution)/shard_map/reduce_scatter | solution.py:50
  8.9 100.6 %copy-start.3 = (bf16[1,256,256]{2,1,0:T(8,128)(2,1)}, bf16[1,256,256]{2,1,0:T(8,128)(2,1)S(1)}, u32[]{:S(2)}) copy-start(bf16[1,256,256]{2,1,0:T(8,128)(2,1)S(1)} %broadcast_select_fusion) | copy-start | bytes 393220
  8.9 38.8 %collective-permute-start = (bf16[1,256,256]{2,1,0:T(8,128)(2,1)S(1)}, bf16[1,256,256]{2,1,0:T(8,128)(2,1)S(1)}, u32[]{:S(2)}, u32[]{:S(2)}) collective-permute-start(bf16[1,256,256]{2,1,0:T(8,128)(2,1)S(1)} %broadcast_select_fusion), channel_id=1, source_target_pairs={{0,16},{2,18},{4,20},{6,22},{8,24},{10,26},{12,28},{14,30},{16,32}... | collective-permute-start | bytes 393224 | tf_op jit(solution)/shard_map/ppermute | solution.py:12
  14.0 40.3 %collective-permute-start.1 = (bf16[1,256,256]{2,1,0:T(8,128)(2,1)S(1)}, bf16[1,256,256]{2,1,0:T(8,128)(2,1)}, u32[]{:S(2)}, u32[]{:S(2)}) collective-permute-start(bf16[1,256,256]{2,1,0:T(8,128)(2,1)S(1)} %broadcast_select_fusion), channel_id=1, source_target_pairs={{0,14},{2,16},{4,18},{6,20},{8,22},{10,24},{12,26},{14,28},{16,30}... | collective-permute-start | bytes 393224 | tf_op jit(solution)/shard_map/ppermute | solution.py:12
  19.4 39.0 %collective-permute-start.2 = (bf16[1,256,256]{2,1,0:T(8,128)(2,1)S(1)}, bf16[1,256,256]{2,1,0:T(8,128)(2,1)}, u32[]{:S(2)}, u32[]{:S(2)}) collective-permute-start(bf16[1,256,256]{2,1,0:T(8,128)(2,1)S(1)} %broadcast_select_fusion), channel_id=1, source_target_pairs={{0,12},{2,14},{4,16},{6,18},{8,20},{10,22},{12,24},{14,26},{16,28}... | collective-permute-start | bytes 393224 | tf_op jit(solution)/shard_map/ppermute | solution.py:12
  24.2 37.1 %collective-permute-start.3 = (bf16[1,256,256]{2,1,0:T(8,128)(2,1)S(1)}, bf16[1,256,256]{2,1,0:T(8,128)(2,1)}, u32[]{:S(2)}, u32[]{:S(2)}) collective-permute-start(bf16[1,256,256]{2,1,0:T(8,128)(2,1)S(1)} %broadcast_select_fusion), channel_id=1, source_target_pairs={{0,10},{2,12},{4,14},{6,16},{8,18},{10,20},{12,22},{14,24},{16,26}... | collective-permute-start | bytes 393224 | tf_op jit(solution)/shard_map/ppermute | solution.py:12
  26.8 44.2 %collective-permute-start.4 = (bf16[1,256,256]{2,1,0:T(8,128)(2,1)S(1)}, bf16[1,256,256]{2,1,0:T(8,128)(2,1)}, u32[]{:S(2)}, u32[]{:S(2)}) collective-permute-start(bf16[1,256,256]{2,1,0:T(8,128)(2,1)S(1)} %broadcast_select_fusion), channel_id=1, source_target_pairs={{0,8},{2,10},{4,12},{6,14},{8,16},{10,18},{12,20},{14,22},{16,24},... | collective-permute-start | bytes 393224 | tf_op jit(solution)/shard_map/ppermute | solution.py:12
  47.7 61.8 %copy-start = (bf16[1,8,256,256]{3,2,1,0:T(8,128)(2,1)S(1)}, bf16[1,8,256,256]{3,2,1,0:T(8,128)(2,1)}, u32[]{:S(2)}) copy-start(bf16[1,8,256,256]{3,2,1,0:T(8,128)(2,1)} %param.10) | copy-start | bytes 3145732
  47.7 0.7 copy-start.5
  48.4 25.9 %collective-permute-start.5 = (bf16[1,256,256]{2,1,0:T(8,128)(2,1)S(1)}, bf16[1,256,256]{2,1,0:T(8,128)(2,1)S(1)}, u32[]{:S(2)}, u32[]{:S(2)}) collective-permute-start(bf16[1,256,256]{2,1,0:T(8,128)(2,1)S(1)} %broadcast_select_fusion), channel_id=1, source_target_pairs={{0,6},{2,8},{4,10},{6,12},{8,14},{10,16},{12,18},{14,20},{16,22},{... | collective-permute-start | bytes 393224 | tf_op jit(solution)/shard_map/ppermute | solution.py:12
  54.3 22.0 %collective-permute-start.6 = (bf16[1,256,256]{2,1,0:T(8,128)(2,1)S(1)}, bf16[1,256,256]{2,1,0:T(8,128)(2,1)S(1)}, u32[]{:S(2)}, u32[]{:S(2)}) collective-permute-start(bf16[1,256,256]{2,1,0:T(8,128)(2,1)S(1)} %broadcast_select_fusion), channel_id=1, source_target_pairs={{0,4},{2,6},{4,8},{6,10},{8,12},{10,14},{12,16},{14,18},{16,20},{1... | collective-permute-start | bytes 393224 | tf_op jit(solution)/shard_map/ppermute | solution.py:12
  58.4 20.9 %collective-permute-start.7 = (bf16[1,256,256]{2,1,0:T(8,128)(2,1)S(1)}, bf16[1,256,256]{2,1,0:T(8,128)(2,1)S(1)}, u32[]{:S(2)}, u32[]{:S(2)}) collective-permute-start(bf16[1,256,256]{2,1,0:T(8,128)(2,1)S(1)} %broadcast_select_fusion), channel_id=1, source_target_pairs={{0,2},{2,4},{4,6},{6,8},{8,10},{10,12},{12,14},{14,16},{16,18},{18... | collective-permute-start | bytes 393224 | tf_op jit(solution)/shard_map/ppermute | solution.py:12
  61.3 23.5 %collective-permute-start.8 = (bf16[1,256,256]{2,1,0:T(8,128)(2,1)S(1)}, bf16[1,256,256]{2,1,0:T(8,128)(2,1)S(1)}, u32[]{:S(2)}, u32[]{:S(2)}) collective-permute-start(bf16[1,256,256]{2,1,0:T(8,128)(2,1)S(1)} %broadcast_select_fusion), channel_id=1, source_target_pairs={{0,510},{2,0},{4,2},{6,4},{8,6},{10,8},{12,10},{14,12},{16,14},{18... | collective-permute-start | bytes 393224 | tf_op jit(solution)/shard_map/ppermute | solution.py:12
  71.0 20.0 %collective-permute-start.9 = (bf16[1,256,256]{2,1,0:T(8,128)(2,1)S(1)}, bf16[1,256,256]{2,1,0:T(8,128)(2,1)S(1)}, u32[]{:S(2)}, u32[]{:S(2)}) collective-permute-start(bf16[1,256,256]{2,1,0:T(8,128)(2,1)S(1)} %broadcast_select_fusion), channel_id=1, source_target_pairs={{0,508},{2,510},{4,0},{6,2},{8,4},{10,6},{12,8},{14,10},{16,12},{1... | collective-permute-start | bytes 393224 | tf_op jit(solution)/shard_map/ppermute | solution.py:12
  74.4 20.1 %collective-permute-start.10 = (bf16[1,256,256]{2,1,0:T(8,128)(2,1)S(1)}, bf16[1,256,256]{2,1,0:T(8,128)(2,1)S(1)}, u32[]{:S(2)}, u32[]{:S(2)}) collective-permute-start(bf16[1,256,256]{2,1,0:T(8,128)(2,1)S(1)} %broadcast_select_fusion), channel_id=1, source_target_pairs={{0,506},{2,508},{4,510},{6,0},{8,2},{10,4},{12,6},{14,8},{16,10},{... | collective-permute-start | bytes 393224 | tf_op jit(solution)/shard_map/ppermute | solution.py:12
  76.3 24.5 %collective-permute-start.11 = (bf16[1,256,256]{2,1,0:T(8,128)(2,1)S(1)}, bf16[1,256,256]{2,1,0:T(8,128)(2,1)S(1)}, u32[]{:S(2)}, u32[]{:S(2)}) collective-permute-start(bf16[1,256,256]{2,1,0:T(8,128)(2,1)S(1)} %broadcast_select_fusion), channel_id=1, source_target_pairs={{0,504},{2,506},{4,508},{6,510},{8,0},{10,2},{12,4},{14,6},{16,8},... | collective-permute-start | bytes 393224 | tf_op jit(solution)/shard_map/ppermute | solution.py:12
  79.3 21.6 %collective-permute-start.12 = (bf16[1,256,256]{2,1,0:T(8,128)(2,1)S(1)}, bf16[1,256,256]{2,1,0:T(8,128)(2,1)S(1)}, u32[]{:S(2)}, u32[]{:S(2)}) collective-permute-start(bf16[1,256,256]{2,1,0:T(8,128)(2,1)S(1)} %broadcast_select_fusion), channel_id=1, source_target_pairs={{0,502},{2,504},{4,506},{6,508},{8,510},{10,0},{12,2},{14,4},{16,6... | collective-permute-start | bytes 393224 | tf_op jit(solution)/shard_map/ppermute | solution.py:12
  84.7 16.1 %collective-permute-start.13 = (bf16[1,256,256]{2,1,0:T(8,128)(2,1)S(1)}, bf16[1,256,256]{2,1,0:T(8,128)(2,1)S(1)}, u32[]{:S(2)}, u32[]{:S(2)}) collective-permute-start(bf16[1,256,256]{2,1,0:T(8,128)(2,1)S(1)} %broadcast_select_fusion), channel_id=1, source_target_pairs={{0,500},{2,502},{4,504},{6,506},{8,508},{10,510},{12,0},{14,2},{16... | collective-permute-start | bytes 393224 | tf_op jit(solution)/shard_map/ppermute | solution.py:12
  91.0 10.1 %collective-permute-start.14 = (bf16[1,256,256]{2,1,0:T(8,128)(2,1)S(1)}, bf16[1,256,256]{2,1,0:T(8,128)(2,1)S(1)}, u32[]{:S(2)}, u32[]{:S(2)}) collective-permute-start(bf16[1,256,256]{2,1,0:T(8,128)(2,1)S(1)} %broadcast_select_fusion), channel_id=1, source_target_pairs={{0,498},{2,500},{4,502},{6,504},{8,506},{10,508},{12,510},{14,0},{... | collective-permute-start | bytes 393224 | tf_op jit(solution)/shard_map/ppermute | solution.py:12
  94.4 15.1 %collective-permute-start.15 = (bf16[1,256,256]{2,1,0:T(8,128)(2,1)S(1)}, bf16[1,256,256]{2,1,0:T(8,128)(2,1)S(1)}, u32[]{:S(2)}, u32[]{:S(2)}) collective-permute-start(bf16[1,256,256]{2,1,0:T(8,128)(2,1)S(1)} %broadcast_select_fusion), channel_id=1, source_target_pairs={{0,496},{2,498},{4,500},{6,502},{8,504},{10,506},{12,508},{14,510}... | collective-permute-start | bytes 393224 | tf_op jit(solution)/shard_map/ppermute | solution.py:12
  109.5 6.2 %copy-start.1 = (bf16[17,256,256]{2,1,0:T(8,128)(2,1)}, bf16[17,256,256]{2,1,0:T(8,128)(2,1)S(1)}, u32[]{:S(2)}) copy-start(bf16[17,256,256]{2,1,0:T(8,128)(2,1)S(1)} %constant_dynamic-update-slice_fusion) | copy-start | bytes 6684676
  117.7 10.7 %copy-start.6 = (f32[1,256]{1,0:T(1,128)S(1)}, f32[1,256]{1,0:T(1,128)}, u32[]{:S(2)}) copy-start(f32[1,256]{1,0:T(1,128)} %param.12) | copy-start | bytes 3076
  119.7 26.6 %copy-start.4 = (bf16[1,256,256]{2,1,0:T(8,128)(2,1)S(1)}, bf16[1,256,256]{2,1,0:T(8,128)(2,1)}, u32[]{:S(2)}) copy-start(bf16[1,256,256]{2,1,0:T(8,128)(2,1)} %copy-done.3) | copy-start | bytes 393220
Sparse Core Ops, SparseCore 0:
  128.5 17.6 reduce-scatter.1
where the time goes:
time: 156 us; the launch traced here: 155 us
  starting transfers between devices  67.6 us (43%)
  between operations  30.9 us (20%)
  waiting for transfers between devices  26.4 us (17%)
  matrix products  18.8 us (12%)
  local copies, waits for them, and re-layouts  7.69 us (5%)
  other arithmetic  3.6 us (2%)
    ppermute x16, starting transfers between devices, shifted(): return lax.ppermute(value, axis, pairs)  67.5 us
    reduce_scatter x1, waiting for transfers between devices, shards(): lax.psum_scatter(partial_sum, 'aux', scatter_dimension=1, tiled=True)  17.7 us
    dot_general x8, matrix products, shards(): jnp.einsum('pad,pbd->pab', half_product, intersection_now, preferred_elem...  15.8 us
    ppermute x16, waiting for transfers between devices, shifted(): return lax.ppermute(value, axis, pairs)  8.61 us
    unnamed x29, local copies, waits for them, and re-layouts  5.37 us
  transfers between devices with their start and end apart: 17, of which 3 were waited for; matrix products, arithmetic and copies ran while one was open for 5% of the time, Pallas kernels for 0%

commit v1 on v0

v1 whole, which is shorter than its diff:
```python
import functools

import jax
import jax.numpy as jnp
from jax import lax
from jax.experimental import pallas as pl
from jax.experimental.pallas import tpu as pltpu
from jax.sharding import PartitionSpec as P

WIN = 8
MESH = pl.DeviceIdType.MESH


def body(
    pairs,
    amp_hbm,
    ranks_hbm,
    nbr_hbm,
    inter_hbm,
    coup_hbm,
    energy_hbm,
    fact_hbm,
    res_ref,
    upd_ref,
    tbuf,
    sbuf,
    fbuf,
    acc,
    send_half,
    recv_half,
    own_rows,
    energy,
    rank_s,
    nbr_s,
    coup_s,
    loc_sem,
    s_send,
    s_recv,
    t_send,
    t_recv,
    r_sem,
):
    width = amp_hbm.shape[1]
    half_w = width // 2
    slots = nbr_hbm.shape[1]
    p = lax.axis_index("pair")
    c = lax.axis_index("aux")
    other = 1 - c
    sibling = (p, other)
    cols = pl.ds(pl.multiple_of(c * half_w, half_w), half_w)

    def local(src, dst, k):
        return pltpu.make_async_copy(src, dst, loc_sem.at[k])

    loads = [
        local(ranks_hbm, rank_s, 0),
        local(amp_hbm.at[0, :, cols], tbuf.at[WIN], 1),
        local(amp_hbm.at[0, cols, :], own_rows, 2),
        local(nbr_hbm.at[0], nbr_s.at[c], 3),
        local(coup_hbm.at[0], coup_s.at[c], 4),
        local(energy_hbm, energy, 5),
        local(fact_hbm.at[0], fbuf, 6),
        local(inter_hbm.at[0], sbuf.at[pl.ds(c * slots, slots)], 7),
    ]
    for copy in loads:
        copy.start()

    barrier = pltpu.get_barrier_semaphore()
    pl.semaphore_signal(barrier, inc=1, device_id=sibling, device_id_type=MESH)
    for step in range(1, WIN + 1):
        for sign in (1, -1):
            peer = lax.rem(p + sign * step + pairs, pairs)
            pl.semaphore_signal(barrier, inc=1, device_id=(peer, c), device_id_type=MESH)

    loads[0].wait()
    loads[1].wait()
    rank = rank_s[0]
    row_id = lax.broadcasted_iota(jnp.int32, (width, half_w), 0)
    col_id = lax.broadcasted_iota(jnp.int32, (width, half_w), 1) + c * half_w
    tbuf[WIN] = jnp.where((row_id < rank) & (col_id < rank), tbuf[WIN].astype(jnp.float32), 0.0).astype(jnp.bfloat16)

    pl.semaphore_wait(barrier, 2 * WIN + 1)

    sends = []
    for step in range(WIN, 0, -1):
        for sign in (1, -1):
            peer = lax.rem(p + sign * step + pairs, pairs)
            place = WIN - sign * step
            sends.append(
                pltpu.make_async_remote_copy(
                    src_ref=tbuf.at[WIN],
                    dst_ref=tbuf.at[place],
                    send_sem=t_send.at[place],
                    recv_sem=t_recv.at[place],
                    device_id=(peer, c),
                    device_id_type=MESH,
                )
            )
    for copy in sends:
        copy.start()
    shares = []
    for k, (src, dst) in enumerate(
        (
            (nbr_hbm.at[0], nbr_s.at[c]),
            (coup_hbm.at[0], coup_s.at[c]),
            (inter_hbm.at[0], sbuf.at[pl.ds(c * slots, slots)]),
        )
    ):
        shares.append(
            pltpu.make_async_remote_copy(
                src_ref=src, dst_ref=dst, send_sem=s_send.at[k], recv_sem=s_recv.at[k],
                device_id=sibling, device_id_type=MESH,
            )
        )
    for copy in shares:
        copy.start()

    loads[6].wait()
    acc[...] = lax.dot_general(
        fbuf[0], fbuf[1], (((0,), (0,)), ((), ())), preferred_element_type=jnp.float32
    )
    for k in (2, 3, 4, 5, 7):
        loads[k].wait()
    for copy in shares:
        copy.wait()

    def couple(w):
        slot = jnp.int32(0)
        factor = jnp.float32(0)
        for core in range(2):
            for n in range(slots):
                hit = lax.rem(nbr_s[core, n] - p + WIN + pairs, pairs) == w
                slot = jnp.where(hit, core * slots + n, slot)
                factor = jnp.where(hit, coup_s[core, n], factor)
        near = sbuf[slot]
        half = jnp.dot(near, tbuf[w], preferred_element_type=jnp.float32).astype(jnp.bfloat16)
        near_cols = sbuf[slot, :, cols]
        projected = lax.dot_general(
            half, near_cols, (((1,), (1,)), ((), ())), preferred_element_type=jnp.float32
        )
        acc[...] += factor * projected

    couple(WIN)

    @pl.loop(0, WIN)
    def _(k):
        step = WIN - k
        for sign in (1, -1):
            place = WIN - sign * step
            pltpu.make_async_copy(tbuf.at[place], tbuf.at[place], t_recv.at[place]).wait()
            couple(place)

    theirs = pl.ds(pl.multiple_of(other * half_w, half_w), half_w)
    send_half[...] = acc[theirs, :]
    ship = pltpu.make_async_remote_copy(
        src_ref=send_half, dst_ref=recv_half, send_sem=r_sem.at[0], recv_sem=r_sem.at[1],
        device_id=sibling, device_id_type=MESH,
    )
    ship.start()
    rows = lax.broadcasted_iota(jnp.int32, (half_w, width), 0) + c * half_w
    columns = lax.broadcasted_iota(jnp.int32, (half_w, width), 1)
    live = (rows < rank) & (columns < rank)
    by_row = jnp.transpose(jnp.broadcast_to(energy[:, cols], (half_w, half_w)))
    denominator = jnp.concatenate([by_row, by_row], axis=1) + energy[...]
    own = jnp.where(live, own_rows[...].astype(jnp.float32), 0.0)
    for copy in sends:
        copy.wait_send()
    ship.wait()
    summed = acc[cols, :] + recv_half[...]
    residual = jnp.where(live, summed + denominator * own, 0.0)
    res_ref[0] = residual
    upd_ref[0] = own - residual / denominator


def shards(amplitudes, ranks, neighbours, intersections, couplings, energies, factors):
    pairs = lax.axis_size("pair")
    width = amplitudes.shape[1]
    half_w = width // 2
    slots = neighbours.shape[1]
    span = factors.shape[2]
    out = jax.ShapeDtypeStruct((1, half_w, width), jnp.float32)
    any_spec = pl.BlockSpec(memory_space=pl.ANY)
    vmem = pl.BlockSpec(memory_space=pltpu.VMEM)
    dma = pltpu.SemaphoreType.DMA
    return pl.pallas_call(
        functools.partial(body, pairs),
        out_shape=(out, out),
        in_specs=[any_spec] * 7,
        out_specs=(vmem, vmem),
        scratch_shapes=[
            pltpu.VMEM((2 * WIN + 1, width, half_w), jnp.bfloat16),
            pltpu.VMEM((2 * slots, width, width), jnp.bfloat16),
            pltpu.VMEM((2, span, width), jnp.bfloat16),
            pltpu.VMEM((width, width), jnp.float32),
            pltpu.VMEM((half_w, width), jnp.float32),
            pltpu.VMEM((half_w, width), jnp.float32),
            pltpu.VMEM((half_w, width), jnp.bfloat16),
            pltpu.VMEM((1, width), jnp.float32),
            pltpu.SMEM((1,), jnp.int32),
            pltpu.SMEM((2, slots), jnp.int32),
            pltpu.SMEM((2, slots), jnp.float32),
            dma((8,)),
            dma((3,)),
            dma((3,)),
            dma((2 * WIN + 1,)),
            dma((2 * WIN + 1,)),
            dma((2,)),
        ],
        compiler_params=pltpu.CompilerParams(
            collective_id=0, has_side_effects=True
        ),
    )(amplitudes, ranks, neighbours, intersections, couplings, energies, factors)


def solution(mesh):
    return jax.shard_map(
        shards,
        mesh=mesh,
        in_specs=(
            P("pair", None, None),
            P("pair"),
            P("pair", "aux"),
            P("pair", "aux", None, None),
            P("pair", "aux"),
            P("pair", None),
            P("pair", None, "aux", None),
        ),
        out_specs=(P("pair", "aux", None), P("pair", "aux", None)),
        check_vma=False,
    )
```

time: 156 us -> 43.2 us (0.28)
  starting transfers between devices: 67.6 us -> 0 us
  Pallas kernels: 0 us -> 38.6 us
  between operations: 30.9 us -> 1.29 us
  waiting for transfers between devices: 26.4 us -> 0 us
  matrix products: 18.8 us -> 0 us
  local copies, waits for them, and re-layouts: 7.69 us -> 3.14 us
  other arithmetic: 3.6 us -> 0 us
    ppermute x16 -> x0, starting transfers between devices: 67.5 us -> none  [shifted(): return lax.ppermute(value, axis, pairs)]
    pallas_call x0 -> x1, Pallas kernels: none -> 38.6 us  [shards(): pl.pallas_call(functools.partial(body, pairs), out_shape=(out, out), in_s...]
    dot_general x9 -> x0, matrix products: 18.8 us -> none  [the longest x8 15.8 us: shards(): jnp.einsum('pad,pbd->pab', half_product, intersection_now, preferred_elem...]
    reduce_scatter x1 -> x0, waiting for transfers between devices: 17.7 us -> none  [shards(): lax.psum_scatter(partial_sum, 'aux', scatter_dimension=1, tiled=True)]
    ppermute x16 -> x0, waiting for transfers between devices: 8.61 us -> none  [shifted(): return lax.ppermute(value, axis, pairs)]
    slice x2 -> x0, local copies, waits for them, and re-layouts: 2.3 us -> none  [the longest x1 1.61 us: shards(): partial_sum = partial_sum + couplings[:, column][:, None, None] * projected]
    unnamed x29 -> x2, local copies, waits for them, and re-layouts: 5.37 us -> 3.14 us
    sub x1 -> x0, other arithmetic: 1.71 us -> none  [shards(): return (residual, row_amp - residual / denominator)]
  transfers between devices with their start and end apart: 17 -> 0, of which waited for: 3 -> 0; matrix products, arithmetic and copies ran while one was open for 5% -> 0% of each run, Pallas kernels for 0% -> 0%
where the time goes in v1:
time: 43.2 us; the launch traced here: 43 us
  Pallas kernels  38.6 us (89%)
  local copies, waits for them, and re-layouts  3.14 us (7%)
  between operations  1.29 us (3%)
    pallas_call x1, Pallas kernels, shards(): pl.pallas_call(functools.partial(body, pairs), out_shape=(out, out), in_s...  38.6 us
    unnamed x2, local copies, waits for them, and re-layouts  3.14 us

profile of v1, /device:TPU:1, one launch (start us, length us, event | category | flops | bytes accessed | tf_op | source)
XLA Modules:
  0.0 43.0 jit_solution(16637659766557203618)
XLA Ops:
  1.3 38.6 %shard_map.86 = (f32[1,128,256]{2,1,0:T(8,128)}, f32[1,128,256]{2,1,0:T(8,128)}) custom-call(bf16[1,256,256]{2,1,0:T(8,128)(2,1)} %amp_hbm.1, s32[1]{0:T(128)S(6)} %copy.11.ranks_hbm, s32[1,8]{1,0:T(1,128)} %nbr_hbm.1, bf16[1,8,256,256]{3,2,1,0:T(8,128)(2,1)} %inter_hbm.1, f32[1,8]{1,0:T(1,128)} %coup_hbm.1, f32[1,256]{1,0:T(1,128)} %energy_hbm.1, ...), custom_call_target="tpu_custom_call" | custom-call | tf_op jit(solution)/shard_map/pallas_call | solution.py:185
  39.9 1.6 %copy.12 = f32[1,128,256]{2,1,0:T(8,128)} copy(f32[1,128,256]{2,1,0:T(8,128)} %get-tuple-element.4) | data formatting | bytes 262144
  41.4 1.6 %copy.13 = f32[1,128,256]{2,1,0:T(8,128)} copy(f32[1,128,256]{2,1,0:T(8,128)} %get-tuple-element.5) | data formatting | bytes 262144

commit v2 on v1

v2 whole, which is shorter than its diff:
```python
import functools

import jax
import jax.numpy as jnp
from jax import lax
from jax.experimental import pallas as pl
from jax.experimental.pallas import tpu as pltpu
from jax.sharding import PartitionSpec as P

WIN = 8
RING = 4
REACH = WIN // RING
MESH = pl.DeviceIdType.MESH


def body(
    pairs,
    amp_hbm,
    ranks_hbm,
    nbr_hbm,
    inter_hbm,
    coup_hbm,
    energy_hbm,
    fact_hbm,
    res_ref,
    upd_ref,
    tbuf,
    sbuf,
    fbuf,
    acc,
    send_half,
    recv_half,
    own_rows,
    energy,
    rank_s,
    nbr_s,
    coup_s,
    slot_s,
    factor_s,
    loc_sem,
    s_send,
    s_recv,
    t_send,
    t_recv,
    r_sem,
):
    width = amp_hbm.shape[1]
    half_w = width // 2
    slots = nbr_hbm.shape[1]
    rows_all = pairs // RING
    p = lax.axis_index("pair")
    c = lax.axis_index("aux")
    other = 1 - c
    sibling = (p, other)
    x = lax.rem(p, RING)
    row = p // RING
    cols = pl.ds(pl.multiple_of(c * half_w, half_w), half_w)

    def column(dx):
        return lax.rem(x + dx + RING, RING)

    def far_row(dy):
        return lax.rem(row + dy + rows_all, rows_all)

    def chip(dx, dy):
        return (far_row(dy) * RING + column(dx), c)

    def local(src, dst, k):
        return pltpu.make_async_copy(src, dst, loc_sem.at[k])

    own_tile = tbuf.at[REACH, x]
    loads = [
        local(ranks_hbm, rank_s, 0),
        local(amp_hbm.at[0, :, cols], own_tile, 1),
        local(nbr_hbm.at[0], nbr_s.at[c], 2),
        local(coup_hbm.at[0], coup_s.at[c], 3),
        local(fact_hbm.at[0], fbuf, 4),
        local(inter_hbm.at[0], sbuf.at[pl.ds(c * slots, slots)], 5),
        local(amp_hbm.at[0, cols, :], own_rows, 6),
        local(energy_hbm, energy, 7),
    ]
    for copy in loads:
        copy.start()

    barrier = pltpu.get_barrier_semaphore()
    row_steps = (1, -1, 2, -2)
    peers = [sibling]
    peers += [chip(0, dy) for dy in row_steps]
    peers += [chip(dx, 0) for dx in (1, 2, 3)]
    for peer in peers:
        pl.semaphore_signal(barrier, inc=1, device_id=peer, device_id_type=MESH)

    loads[0].wait()
    loads[1].wait()
    rank = rank_s[0]
    row_id = lax.broadcasted_iota(jnp.int32, (width, half_w), 0)
    col_id = lax.broadcasted_iota(jnp.int32, (width, half_w), 1) + c * half_w
    own_tile[...] = jnp.where(
        (row_id < rank) & (col_id < rank), own_tile[...].astype(jnp.float32), 0.0
    ).astype(jnp.bfloat16)

    pl.semaphore_wait(barrier, len(peers))

    def send(tile, home, k, peer):
        return pltpu.make_async_remote_copy(
            src_ref=tile,
            dst_ref=tbuf.at[home],
            send_sem=t_send.at[k],
            recv_sem=t_recv.at[home],
            device_id=peer,
            device_id_type=MESH,
        )

    first = []
    for dy in row_steps:
        first.append(send(own_tile, (REACH - dy, x), len(first), chip(0, dy)))
    for dx in (1, 3, 2):
        first.append(send(own_tile, (REACH, x), len(first), chip(dx, 0)))
    for copy in first:
        copy.start()

    shares = []
    for k, (src, dst) in enumerate(
        (
            (nbr_hbm.at[0], nbr_s.at[c]),
            (coup_hbm.at[0], coup_s.at[c]),
            (inter_hbm.at[0], sbuf.at[pl.ds(c * slots, slots)]),
        )
    ):
        shares.append(
            pltpu.make_async_remote_copy(
                src_ref=src, dst_ref=dst, send_sem=s_send.at[k], recv_sem=s_recv.at[k],
                device_id=sibling, device_id_type=MESH,
            )
        )
    for copy in shares:
        copy.start()

    for k in (4, 2, 3, 5, 6, 7):
        loads[k].wait()
    acc[...] = lax.dot_general(
        fbuf[0], fbuf[1], (((0,), (0,)), ((), ())), preferred_element_type=jnp.float32
    )
    for copy in shares:
        copy.wait()

    for r in range(2 * REACH + 1):
        for xs in range(RING):
            q = far_row(r - REACH) * RING + xs
            slot = jnp.int32(0)
            factor = jnp.float32(0)
            for core in range(2):
                for n in range(slots):
                    hit = nbr_s[core, n] == q
                    slot = jnp.where(hit, core * slots + n, slot)
                    factor = jnp.where(hit, coup_s[core, n], factor)
            slot_s[r, xs] = slot
            factor_s[r, xs] = factor

    def arrived(r, xs):
        tile = tbuf.at[r, xs]
        pltpu.make_async_copy(tile, tile, t_recv.at[r, xs]).wait()

    def wanted(r, source, dest):
        if r == 0:
            return dest < source
        if r == 2 * REACH:
            return dest > source
        return None

    def under(condition, act):
        if condition is None:
            act()
        else:
            pl.when(condition)(act)

    def relay_copies(r):
        base = len(first) + 3 * (r if r < REACH else r - 1)
        return [
            (wanted(r, x, column(dx)), send(tbuf.at[r, x], (r, x), base + k, chip(dx, 0)))
            for k, dx in enumerate((1, 3, 2))
        ]

    def relay(r):
        arrived(r, x)
        for condition, copy in relay_copies(r):
            under(condition, copy.start)

    def couple(r, xs):
        slot = slot_s[r, xs]
        near = sbuf[slot]
        half = jnp.dot(near, tbuf[r, xs], preferred_element_type=jnp.float32).astype(jnp.bfloat16)
        projected = lax.dot_general(
            half, sbuf[slot, :, cols], (((1,), (1,)), ((), ())), preferred_element_type=jnp.float32
        )
        acc[...] += factor_s[r, xs] * projected

    early = row < REACH

    def couple_row(r):
        if r != REACH:
            couple(r, x)

        @pl.loop(1, RING)
        def _(k):
            dx = jnp.where(k == 1, 1, jnp.where(k == 2, 3, 2))
            xs = column(dx)

            def act():
                arrived(r, xs)
                couple(r, xs)

            under(wanted(r, xs, x), act)

    relay(REACH + 1)
    relay(REACH + 2)

    @pl.when(jnp.logical_not(early))
    def _():
        relay(REACH - 1)
        relay(REACH - 2)

    couple(REACH, x)
    couple_row(REACH)
    couple_row(REACH + 1)
    couple_row(REACH + 2)

    @pl.when(early)
    def _():
        relay(REACH - 1)
        relay(REACH - 2)

    couple_row(REACH - 1)
    couple_row(REACH - 2)

    theirs = pl.ds(pl.multiple_of(other * half_w, half_w), half_w)
    send_half[...] = acc[theirs, :]
    ship = pltpu.make_async_remote_copy(
        src_ref=send_half, dst_ref=recv_half, send_sem=r_sem.at[0], recv_sem=r_sem.at[1],
        device_id=sibling, device_id_type=MESH,
    )
    ship.start()
    rows = lax.broadcasted_iota(jnp.int32, (half_w, width), 0) + c * half_w
    columns = lax.broadcasted_iota(jnp.int32, (half_w, width), 1)
    live = (rows < rank) & (columns < rank)
    by_row = jnp.transpose(jnp.broadcast_to(energy[:, cols], (half_w, half_w)))
    denominator = jnp.concatenate([by_row, by_row], axis=1) + energy[...]
    own = jnp.where(live, own_rows[...].astype(jnp.float32), 0.0)
    for copy in first:
        copy.wait_send()
    for r in (REACH + 1, REACH + 2, REACH - 1, REACH - 2):
        for condition, copy in relay_copies(r):
            under(condition, copy.wait_send)
    ship.wait()
    summed = acc[cols, :] + recv_half[...]
    residual = jnp.where(live, summed + denominator * own, 0.0)
    res_ref[0] = residual
    upd_ref[0] = own - residual / denominator


def shards(amplitudes, ranks, neighbours, intersections, couplings, energies, factors):
    pairs = lax.axis_size("pair")
    width = amplitudes.shape[1]
    half_w = width // 2
    slots = neighbours.shape[1]
    span = factors.shape[2]
    out = jax.ShapeDtypeStruct((1, half_w, width), jnp.float32)
    hbm = pl.BlockSpec(memory_space=pltpu.HBM)
    vmem = pl.BlockSpec(memory_space=pltpu.VMEM)
    dma = pltpu.SemaphoreType.DMA
    tiles = (2 * REACH + 1, RING)
    return pl.pallas_call(
        functools.partial(body, pairs),
        out_shape=(out, out),
        in_specs=[hbm] * 7,
        out_specs=(vmem, vmem),
        scratch_shapes=[
            pltpu.VMEM(tiles + (width, half_w), jnp.bfloat16),
            pltpu.VMEM((2 * slots, width, width), jnp.bfloat16),
            pltpu.VMEM((2, span, width), jnp.bfloat16),
            pltpu.VMEM((width, width), jnp.float32),
            pltpu.VMEM((half_w, width), jnp.float32),
            pltpu.VMEM((half_w, width), jnp.float32),
            pltpu.VMEM((half_w, width), jnp.bfloat16),
            pltpu.VMEM((1, width), jnp.float32),
            pltpu.SMEM((1,), jnp.int32),
            pltpu.SMEM((2, slots), jnp.int32),
            pltpu.SMEM((2, slots), jnp.float32),
            pltpu.SMEM(tiles, jnp.int32),
            pltpu.SMEM(tiles, jnp.float32),
            dma((8,)),
            dma((3,)),
            dma((3,)),
            dma((7 + 3 * 2 * REACH,)),
            dma(tiles),
            dma((2,)),
        ],
        compiler_params=pltpu.CompilerParams(
            collective_id=0, has_side_effects=True, vmem_limit_bytes=VMEM_LIMIT
        ),
    )(amplitudes, ranks, neighbours, intersections, couplings, energies, factors)


VMEM_LIMIT = 56000000


def solution(mesh):
    return jax.shard_map(
        shards,
        mesh=mesh,
        in_specs=(
            P("pair", None, None),
            P("pair"),
            P("pair", "aux"),
            P("pair", "aux", None, None),
            P("pair", "aux"),
            P("pair", None),
            P("pair", None, "aux", None),
        ),
        out_specs=(P("pair", "aux", None), P("pair", "aux", None)),
        check_vma=False,
    )
```

time: 43.2 us -> 42.6 us (0.986)
  Pallas kernels: 38.6 us -> 36.9 us
  local copies, waits for them, and re-layouts: 3.14 us -> 4.2 us
    pallas_call x1, Pallas kernels: 38.6 us -> 36.9 us  [shards(): pl.pallas_call(functools.partial(body, pairs), out_shape=(out, out), in_s...]
    unnamed x2 -> x10, local copies, waits for them, and re-layouts: 3.14 us -> 4.2 us
where the time goes in v2:
time: 42.6 us; the launch traced here: 42.4 us
  Pallas kernels  36.9 us (87%)
  local copies, waits for them, and re-layouts  4.2 us (10%)
  between operations  1.3 us (3%)
    pallas_call x1, Pallas kernels, shards(): pl.pallas_call(functools.partial(body, pairs), out_shape=(out, out), in_s...  36.9 us
    unnamed x10, local copies, waits for them, and re-layouts  4.2 us

profile of v2, /device:TPU:1, one launch (start us, length us, event | category | flops | bytes accessed | tf_op | source)
XLA Modules:
  0.0 42.4 jit_solution(9456848980353788880)
XLA Ops:
  1.3 0.0 copy-start
  1.3 0.9 %copy-done = bf16[1,256,256]{2,1,0:T(8,128)(2,1)S(1)} copy-done((bf16[1,256,256]{2,1,0:T(8,128)(2,1)S(1)}, bf16[1,256,256]{2,1,0:T(8,128)(2,1)}, u32[]{:S(2)}) %copy-start) | copy-done | bytes 131096
  2.2 0.0 copy-start.1
  2.2 0.7 %copy-done.1 = f32[1,256]{1,0:T(1,128)S(1)} copy-done((f32[1,256]{1,0:T(1,128)S(1)}, f32[1,256]{1,0:T(1,128)}, u32[]{:S(2)}) %copy-start.1) | copy-done | bytes 1048
  2.9 0.0 copy-start.2
  2.9 0.7 %copy-done.2 = s32[1,8]{1,0:T(1,128)S(1)} copy-done((s32[1,8]{1,0:T(1,128)S(1)}, s32[1,8]{1,0:T(1,128)}, u32[]{:S(2)}) %copy-start.2) | copy-done | bytes 56
  3.5 0.0 copy-start.3
  3.5 0.7 %copy-done.3 = f32[1,8]{1,0:T(1,128)S(1)} copy-done((f32[1,8]{1,0:T(1,128)S(1)}, f32[1,8]{1,0:T(1,128)}, u32[]{:S(2)}) %copy-start.3) | copy-done | bytes 56
  4.2 36.9 %shard_map.86 = (f32[1,128,256]{2,1,0:T(8,128)S(1)}, f32[1,128,256]{2,1,0:T(8,128)S(1)}) custom-call(bf16[1,256,256]{2,1,0:T(8,128)(2,1)S(1)} %copy-done, s32[1]{0:T(128)S(6)} %copy.11.ranks_hbm, s32[1,8]{1,0:T(1,128)S(1)} %copy-done.2, bf16[1,8,256,256]{3,2,1,0:T(8,128)(2,1)} %inter_hbm.1, f32[1,8]{1,0:T(1,128)S(1)} %copy-done.3, f32[1,256]{1,0:T(1,128)S(1)} %copy-done.1, ...), custom_call_target="tpu_custom_call" | custom-call | tf_op jit(solution)/shard_map/pallas_call | solution.py:272
  41.1 0.7 %copy.12 = f32[1,128,256]{2,1,0:T(8,128)} copy(f32[1,128,256]{2,1,0:T(8,128)S(1)} %get-tuple-element.4) | data formatting | bytes 262144
  41.7 0.7 %copy.13 = f32[1,128,256]{2,1,0:T(8,128)} copy(f32[1,128,256]{2,1,0:T(8,128)S(1)} %get-tuple-element.5) | data formatting | bytes 262144
Async XLA Ops:
  1.3 0.9 %copy-start = (bf16[1,256,256]{2,1,0:T(8,128)(2,1)S(1)}, bf16[1,256,256]{2,1,0:T(8,128)(2,1)}, u32[]{:S(2)}) copy-start(bf16[1,256,256]{2,1,0:T(8,128)(2,1)} %amp_hbm.1) | copy-start | bytes 393220
  2.2 0.7 %copy-start.1 = (f32[1,256]{1,0:T(1,128)S(1)}, f32[1,256]{1,0:T(1,128)}, u32[]{:S(2)}) copy-start(f32[1,256]{1,0:T(1,128)} %energy_hbm.1) | copy-start | bytes 3076
  2.9 0.7 %copy-start.2 = (s32[1,8]{1,0:T(1,128)S(1)}, s32[1,8]{1,0:T(1,128)}, u32[]{:S(2)}) copy-start(s32[1,8]{1,0:T(1,128)} %nbr_hbm.1) | copy-start | bytes 100
  3.5 0.7 %copy-start.3 = (f32[1,8]{1,0:T(1,128)S(1)}, f32[1,8]{1,0:T(1,128)}, u32[]{:S(2)}) copy-start(f32[1,8]{1,0:T(1,128)} %coup_hbm.1) | copy-start | bytes 100

commit v3 on v2

--- a/solution.py
+++ b/solution.py
@@ -32,7 +32,6 @@
     recv_half,
     own_rows,
     energy,
-    rank_s,
     nbr_s,
     coup_s,
     slot_s,
@@ -43,6 +42,7 @@
     t_send,
     t_recv,
     r_sem,
+    hello,
 ):
     width = amp_hbm.shape[1]
     half_w = width // 2
@@ -70,36 +70,32 @@
 
     own_tile = tbuf.at[REACH, x]
     loads = [
-        local(ranks_hbm, rank_s, 0),
+        local(energy_hbm, energy, 0),
         local(amp_hbm.at[0, :, cols], own_tile, 1),
         local(nbr_hbm.at[0], nbr_s.at[c], 2),
         local(coup_hbm.at[0], coup_s.at[c], 3),
         local(fact_hbm.at[0], fbuf, 4),
         local(inter_hbm.at[0], sbuf.at[pl.ds(c * slots, slots)], 5),
         local(amp_hbm.at[0, cols, :], own_rows, 6),
-        local(energy_hbm, energy, 7),
     ]
     for copy in loads:
         copy.start()
 
     barrier = pltpu.get_barrier_semaphore()
-    row_steps = (1, -1, 2, -2)
-    peers = [sibling]
-    peers += [chip(0, dy) for dy in row_steps]
-    peers += [chip(dx, 0) for dx in (1, 2, 3)]
-    for peer in peers:
+    callers = [sibling, chip(0, -1), chip(0, -2)]
+    callers += [chip(dx, 0) for dx in (1, 2, 3)]
+    for peer in callers:
         pl.semaphore_signal(barrier, inc=1, device_id=peer, device_id_type=MESH)
 
-    loads[0].wait()
     loads[1].wait()
-    rank = rank_s[0]
+    rank = ranks_hbm[0]
     row_id = lax.broadcasted_iota(jnp.int32, (width, half_w), 0)
     col_id = lax.broadcasted_iota(jnp.int32, (width, half_w), 1) + c * half_w
     own_tile[...] = jnp.where(
         (row_id < rank) & (col_id < rank), own_tile[...].astype(jnp.float32), 0.0
     ).astype(jnp.bfloat16)
 
-    pl.semaphore_wait(barrier, len(peers))
+    pl.semaphore_wait(barrier, len(callers))
 
     def send(tile, home, k, peer):
         return pltpu.make_async_remote_copy(
@@ -111,13 +107,20 @@
             device_id_type=MESH,
         )
 
-    first = []
-    for dy in row_steps:
-        first.append(send(own_tile, (REACH - dy, x), len(first), chip(0, dy)))
-    for dx in (1, 3, 2):
-        first.append(send(own_tile, (REACH, x), len(first), chip(dx, 0)))
-    for copy in first:
-        copy.start()
+    up = [send(own_tile, (REACH - dy, x), dy - 1, chip(0, dy)) for dy in (1, 2)]
+    down = [send(own_tile, (REACH + dy, x), 1 + dy, chip(0, -dy)) for dy in (1, 2)]
+    side = [send(own_tile, (REACH, x), 3 + dx, chip(dx, 0)) for dx in (1, 3, 2)]
+    first = up + side + down
+    for copy in up:
+        copy.start()
+    for dy in (1, 2):
+        pl.semaphore_signal(hello.at[dy - 1], inc=1, device_id=chip(0, dy), device_id_type=MESH)
+    for copy in side:
+        copy.start()
+
+    def send_down(dy):
+        pl.semaphore_wait(hello.at[dy - 1], 1)
+        down[dy - 1].start()
 
     shares = []
     for k, (src, dst) in enumerate(
@@ -136,11 +139,15 @@
     for copy in shares:
         copy.start()
 
-    for k in (4, 2, 3, 5, 6, 7):
+    for k in (4, 2, 3, 5, 6, 0):
         loads[k].wait()
     acc[...] = lax.dot_general(
         fbuf[0], fbuf[1], (((0,), (0,)), ((), ())), preferred_element_type=jnp.float32
     )
+
+    late = [row < dy for dy in (1, 2)]
+    for dy in (1, 2):
+        pl.when(jnp.logical_not(late[dy - 1]))(functools.partial(send_down, dy))
     for copy in shares:
         copy.wait()
 
@@ -175,7 +182,7 @@
             pl.when(condition)(act)
 
     def relay_copies(r):
-        base = len(first) + 3 * (r if r < REACH else r - 1)
+        base = 7 + 3 * (r if r < REACH else r - 1)
         return [
             (wanted(r, x, column(dx)), send(tbuf.at[r, x], (r, x), base + k, chip(dx, 0)))
             for k, dx in enumerate((1, 3, 2))
@@ -195,8 +202,6 @@
         )
         acc[...] += factor_s[r, xs] * projected
 
-    early = row < REACH
-
     def couple_row(r):
         if r != REACH:
             couple(r, x)
@@ -215,20 +220,18 @@
     relay(REACH + 1)
     relay(REACH + 2)
 
-    @pl.when(jnp.logical_not(early))
-    def _():
-        relay(REACH - 1)
-        relay(REACH - 2)
+    for dy in (1, 2):
+        pl.when(jnp.logical_not(late[dy - 1]))(functools.partial(relay, REACH - dy))
 
     couple(REACH, x)
     couple_row(REACH)
     couple_row(REACH + 1)
     couple_row(REACH + 2)
 
-    @pl.when(early)
-    def _():
-        relay(REACH - 1)
-        relay(REACH - 2)
+    for dy in (1, 2):
+        pl.when(late[dy - 1])(functools.partial(send_down, dy))
+    for dy in (1, 2):
+        pl.when(late[dy - 1])(functools.partial(relay, REACH - dy))
 
     couple_row(REACH - 1)
     couple_row(REACH - 2)
@@ -258,6 +261,17 @@
     upd_ref[0] = own - residual / denominator
 
 
+def store(res_ref, upd_ref, res_hbm, upd_hbm, sem):
+    copies = [
+        pltpu.make_async_copy(src, dst, sem.at[k])
+        for k, (src, dst) in enumerate(((res_ref, res_hbm), (upd_ref, upd_hbm)))
+    ]
+    for copy in copies:
+        copy.start()
+    for copy in copies:
+        copy.wait()
+
+
 def shards(amplitudes, ranks, neighbours, intersections, couplings, energies, factors):
     pairs = lax.axis_size("pair")
     width = amplitudes.shape[1]
@@ -269,10 +283,10 @@
     vmem = pl.BlockSpec(memory_space=pltpu.VMEM)
     dma = pltpu.SemaphoreType.DMA
     tiles = (2 * REACH + 1, RING)
-    return pl.pallas_call(
+    results = pl.pallas_call(
         functools.partial(body, pairs),
         out_shape=(out, out),
-        in_specs=[hbm] * 7,
+        in_specs=[hbm, pl.BlockSpec(memory_space=pltpu.SMEM)] + [hbm] * 5,
         out_specs=(vmem, vmem),
         scratch_shapes=[
             pltpu.VMEM(tiles + (width, half_w), jnp.bfloat16),
@@ -283,25 +297,34 @@
             pltpu.VMEM((half_w, width), jnp.float32),
             pltpu.VMEM((half_w, width), jnp.bfloat16),
             pltpu.VMEM((1, width), jnp.float32),
-            pltpu.SMEM((1,), jnp.int32),
             pltpu.SMEM((2, slots), jnp.int32),
             pltpu.SMEM((2, slots), jnp.float32),
             pltpu.SMEM(tiles, jnp.int32),
             pltpu.SMEM(tiles, jnp.float32),
-            dma((8,)),
+            dma((7,)),
             dma((3,)),
             dma((3,)),
             dma((7 + 3 * 2 * REACH,)),
             dma(tiles),
             dma((2,)),
+            pltpu.SemaphoreType.REGULAR((2,)),
         ],
         compiler_params=pltpu.CompilerParams(
             collective_id=0, has_side_effects=True, vmem_limit_bytes=VMEM_LIMIT
         ),
-    )(amplitudes, ranks, neighbours, intersections, couplings, energies, factors)
-
-
-VMEM_LIMIT = 56000000
+    )(*[a if a.ndim == 1 else pltpu.with_memory_space_constraint(a, pltpu.HBM) for a in (amplitudes, ranks, neighbours, intersections, couplings, energies, factors)])
+
+    return pl.pallas_call(
+        store,
+        out_shape=(out, out),
+        in_specs=[vmem, vmem],
+        out_specs=(hbm, hbm),
+        scratch_shapes=[dma((2,))],
+        compiler_params=pltpu.CompilerParams(vmem_limit_bytes=1 << 20),
+    )(*results)
+
+
+VMEM_LIMIT = 12000000
 
 
 def solution(mesh):

time: 42.6 us -> 33.2 us (0.78)
  Pallas kernels: 36.9 us -> 31.7 us
  local copies, waits for them, and re-layouts: 4.2 us -> 0 us
    pallas_call x1, Pallas kernels: 36.9 us -> 31 us  [shards(): pl.pallas_call(functools.partial(body, pairs), out_shape=(out, out), in_s...]
    unnamed x10 -> x0, local copies, waits for them, and re-layouts: 4.2 us -> none
    pallas_call x0 -> x1, Pallas kernels: none -> 0.72 us  [shards(): pl.pallas_call(store, out_shape=(out, out), in_specs=[vmem, vmem], out_sp...]
where the time goes in v3:
time: 33.2 us; the launch traced here: 33 us
  Pallas kernels  31.7 us (95%)
  between operations  1.28 us (4%)
    pallas_call x1, Pallas kernels, shards(): pl.pallas_call(functools.partial(body, pairs), out_shape=(out, out), in_s...  31 us
    pallas_call x1, Pallas kernels, shards(): pl.pallas_call(store, out_shape=(out, out), in_specs=[vmem, vmem], out_sp...  0.72 us

profile of v3, /device:TPU:1, one launch (start us, length us, event | category | flops | bytes accessed | tf_op | source)
XLA Modules:
  0.0 33.0 jit_solution(5577003241319882441)
XLA Ops:
  1.3 31.0 %shard_map.86 = (f32[1,128,256]{2,1,0:T(8,128)S(1)}, f32[1,128,256]{2,1,0:T(8,128)S(1)}) custom-call(bf16[1,256,256]{2,1,0:T(8,128)(2,1)} %amp_hbm.1, s32[1]{0:T(128)S(6)} %copy.9.ranks_hbm, s32[1,8]{1,0:T(1,128)} %nbr_hbm.1, bf16[1,8,256,256]{3,2,1,0:T(8,128)(2,1)} %inter_hbm.1, f32[1,8]{1,0:T(1,128)} %coup_hbm.1, f32[1,256]{1,0:T(1,128)} %energy_hbm.1, ...), custom_call_target="tpu_custom_call" | custom-call | tf_op jit(solution)/shard_map/pallas_call | solution.py:286
  32.3 0.7 %shard_map.87 = (f32[1,128,256]{2,1,0:T(8,128)}, f32[1,128,256]{2,1,0:T(8,128)}) custom-call(f32[1,128,256]{2,1,0:T(8,128)S(1)} %get-tuple-element.4.res_ref, f32[1,128,256]{2,1,0:T(8,128)S(1)} %get-tuple-element.5.upd_ref), custom_call_target="tpu_custom_call" | custom-call | tf_op jit(solution)/shard_map/pallas_call | solution.py:317

commit v4 on v3

--- a/solution.py
+++ b/solution.py
@@ -10,6 +10,7 @@
 WIN = 8
 RING = 4
 REACH = WIN // RING
+PIECES = 2
 MESH = pl.DeviceIdType.MESH
 
 
@@ -97,30 +98,45 @@
 
     pl.semaphore_wait(barrier, len(callers))
 
-    def send(tile, home, k, peer):
-        return pltpu.make_async_remote_copy(
-            src_ref=tile,
-            dst_ref=tbuf.at[home],
-            send_sem=t_send.at[k],
-            recv_sem=t_recv.at[home],
-            device_id=peer,
-            device_id_type=MESH,
-        )
-
-    up = [send(own_tile, (REACH - dy, x), dy - 1, chip(0, dy)) for dy in (1, 2)]
-    down = [send(own_tile, (REACH + dy, x), 1 + dy, chip(0, -dy)) for dy in (1, 2)]
-    side = [send(own_tile, (REACH, x), 3 + dx, chip(dx, 0)) for dx in (1, 3, 2)]
-    first = up + side + down
-    for copy in up:
-        copy.start()
+    def piece(r, xs, h):
+        return tbuf.at[r, xs, pl.ds(h * (width // PIECES), width // PIECES)]
+
+    def send(r, xs, home, k, peer):
+        return [
+            pltpu.make_async_remote_copy(
+                src_ref=piece(r, xs, h),
+                dst_ref=piece(home, xs, h),
+                send_sem=t_send.at[k, h],
+                recv_sem=t_recv.at[home, xs, h],
+                device_id=peer,
+                device_id_type=MESH,
+            )
+            for h in range(PIECES)
+        ]
+
+    def start(copies):
+        for copy in copies:
+            copy.start()
+
+    top = rows_all - 1
+    across = column(2)
+    lead = jnp.where(row == top, 1, 2)
+    up = [send(REACH, x, REACH - dy, dy - 1, chip(0, dy)) for dy in (lead, 3 - lead)]
+    down = [send(REACH, x, REACH + dy, 1 + dy, chip(0, -dy)) for dy in (1, 2)]
+    side = [send(REACH, x, REACH, 3 + dx, chip(dx, 0)) for dx in (2, 1, 3)]
+    pass_up = send(REACH, across, REACH - 1, 7, chip(0, 1))
+    pass_down = send(REACH, across, REACH + 1, 8, chip(0, -1))
+    first = up + side + down + [pass_up, pass_down]
+    for copies in up:
+        start(copies)
     for dy in (1, 2):
         pl.semaphore_signal(hello.at[dy - 1], inc=1, device_id=chip(0, dy), device_id_type=MESH)
-    for copy in side:
-        copy.start()
+    for copies in side:
+        start(copies)
 
     def send_down(dy):
         pl.semaphore_wait(hello.at[dy - 1], 1)
-        down[dy - 1].start()
+        start(down[dy - 1])
 
     shares = []
     for k, (src, dst) in enumerate(
@@ -145,9 +161,17 @@
         fbuf[0], fbuf[1], (((0,), (0,)), ((), ())), preferred_element_type=jnp.float32
     )
 
-    late = [row < dy for dy in (1, 2)]
-    for dy in (1, 2):
-        pl.when(jnp.logical_not(late[dy - 1]))(functools.partial(send_down, dy))
+    side_of = jnp.where(row < REACH, 1, -1)
+
+    def late(dy):
+        low = (row < dy) & ((row > 0) | (c == 1))
+        return low | (top - row < dy)
+
+    def soon(dy):
+        return jnp.logical_not(late(dy))
+
+    for dy in (1, 2):
+        pl.when(jnp.logical_not(row < dy))(functools.partial(send_down, dy))
     for copy in shares:
         copy.wait()
 
@@ -164,77 +188,81 @@
             slot_s[r, xs] = slot
             factor_s[r, xs] = factor
 
-    def arrived(r, xs):
-        tile = tbuf.at[r, xs]
-        pltpu.make_async_copy(tile, tile, t_recv.at[r, xs]).wait()
+    def arrived(r, xs, pieces=range(PIECES)):
+        for h in pieces:
+            part = piece(r, xs, h)
+            pltpu.make_async_copy(part, part, t_recv.at[r, xs, h]).wait()
 
     def wanted(r, source, dest):
-        if r == 0:
-            return dest < source
-        if r == 2 * REACH:
-            return dest > source
-        return None
-
-    def under(condition, act):
-        if condition is None:
-            act()
-        else:
-            pl.when(condition)(act)
+        return ((r > 0) | (dest <= source)) & ((r < 2 * REACH) | (dest >= source))
 
     def relay_copies(r):
-        base = 7 + 3 * (r if r < REACH else r - 1)
-        return [
-            (wanted(r, x, column(dx)), send(tbuf.at[r, x], (r, x), base + k, chip(dx, 0)))
-            for k, dx in enumerate((1, 3, 2))
-        ]
+        outer = (r == 0) | (r == 2 * REACH)
+        copies = []
+        for k, dx in enumerate((2, 1, 3)):
+            needed = wanted(r, x, column(dx))
+            if dx == 2:
+                needed &= outer
+            copies.append((needed, send(r, x, r, 9 + 3 * r + k, chip(dx, 0))))
+        return copies
 
     def relay(r):
-        arrived(r, x)
-        for condition, copy in relay_copies(r):
-            under(condition, copy.start)
-
-    def couple(r, xs):
-        slot = slot_s[r, xs]
-        near = sbuf[slot]
-        half = jnp.dot(near, tbuf[r, xs], preferred_element_type=jnp.float32).astype(jnp.bfloat16)
-        projected = lax.dot_general(
-            half, sbuf[slot, :, cols], (((1,), (1,)), ((), ())), preferred_element_type=jnp.float32
-        )
-        acc[...] += factor_s[r, xs] * projected
+        copies = relay_copies(r)
+        for h in range(PIECES):
+            arrived(r, x, (h,))
+            for needed, parts in copies:
+                pl.when(needed)(parts[h].start)
 
     def couple_row(r):
-        if r != REACH:
-            couple(r, x)
-
-        @pl.loop(1, RING)
-        def _(k):
-            dx = jnp.where(k == 1, 1, jnp.where(k == 2, 3, 2))
+        picks = []
+        for dx in (0, 1, 3, 2):
             xs = column(dx)
-
-            def act():
-                arrived(r, xs)
-                couple(r, xs)
-
-            under(wanted(r, xs, x), act)
-
-    relay(REACH + 1)
-    relay(REACH + 2)
-
-    for dy in (1, 2):
-        pl.when(jnp.logical_not(late[dy - 1]))(functools.partial(relay, REACH - dy))
-
-    couple(REACH, x)
-    couple_row(REACH)
-    couple_row(REACH + 1)
-    couple_row(REACH + 2)
-
-    for dy in (1, 2):
-        pl.when(late[dy - 1])(functools.partial(send_down, dy))
-    for dy in (1, 2):
-        pl.when(late[dy - 1])(functools.partial(relay, REACH - dy))
-
-    couple_row(REACH - 1)
-    couple_row(REACH - 2)
+            if dx == 0:
+                picks.append((xs, factor_s[r, xs]))
+            else:
+                needed = wanted(r, xs, x)
+                due = needed & (r != REACH) if dx == 2 else needed
+                pl.when(due)(functools.partial(arrived, r, xs))
+                picks.append((jnp.where(needed, xs, x), jnp.where(needed, factor_s[r, xs], 0.0)))
+        total = acc[...]
+        for xs, factor in picks:
+            slot = slot_s[r, xs]
+            half = jnp.dot(
+                sbuf[slot], tbuf[r, xs], preferred_element_type=jnp.float32
+            ).astype(jnp.bfloat16)
+            total += factor * lax.dot_general(
+                half, sbuf[slot, :, cols], (((1,), (1,)), ((), ())), preferred_element_type=jnp.float32
+            )
+        acc[...] = total
+
+    arrived(REACH, across)
+    start(pass_up)
+    pl.when(row > 0)(functools.partial(start, pass_down))
+    for dy in (1, 2):
+        relay(REACH + dy * side_of)
+
+    def other_side(dy):
+        def release():
+            send_down(dy)
+            if dy == 1:
+                start(pass_down)
+
+        pl.when(row < dy)(release)
+        relay(REACH - dy * side_of)
+
+    for dy in (1, 2):
+        pl.when(soon(dy))(functools.partial(other_side, dy))
+
+    @pl.loop(0, REACH + 1)
+    def _(k):
+        couple_row(REACH + k * side_of)
+
+    for dy in (1, 2):
+        pl.when(late(dy))(functools.partial(other_side, dy))
+
+    @pl.loop(1, REACH + 1)
+    def _(k):
+        couple_row(REACH - k * side_of)
 
     theirs = pl.ds(pl.multiple_of(other * half_w, half_w), half_w)
     send_half[...] = acc[theirs, :]
@@ -249,11 +277,18 @@
     by_row = jnp.transpose(jnp.broadcast_to(energy[:, cols], (half_w, half_w)))
     denominator = jnp.concatenate([by_row, by_row], axis=1) + energy[...]
     own = jnp.where(live, own_rows[...].astype(jnp.float32), 0.0)
-    for copy in first:
-        copy.wait_send()
-    for r in (REACH + 1, REACH + 2, REACH - 1, REACH - 2):
-        for condition, copy in relay_copies(r):
-            under(condition, copy.wait_send)
+    for copies in first:
+        for copy in copies:
+            copy.wait_send()
+
+    @pl.loop(0, 2 * REACH + 1)
+    def _(r):
+        for needed, copies in relay_copies(r):
+            @pl.when(needed & (r != REACH))
+            def _(copies=copies):
+                for copy in copies:
+                    copy.wait_send()
+
     ship.wait()
     summed = acc[cols, :] + recv_half[...]
     residual = jnp.where(live, summed + denominator * own, 0.0)
@@ -304,8 +339,8 @@
             dma((7,)),
             dma((3,)),
             dma((3,)),
-            dma((7 + 3 * 2 * REACH,)),
-            dma(tiles),
+            dma((9 + 3 * (2 * REACH + 1), PIECES)),
+            dma(tiles + (PIECES,)),
             dma((2,)),
             pltpu.SemaphoreType.REGULAR((2,)),
         ],

time: 33.2 us -> 29.8 us (0.90)
  Pallas kernels: 31.7 us -> 28.3 us
    pallas_call x1, Pallas kernels: 31 us -> 27.6 us  [shards(): pl.pallas_call(functools.partial(body, pairs), out_shape=(out, out), in_s...]
where the time goes in v4:
time: 29.8 us; the launch traced here: 29.6 us
  Pallas kernels  28.3 us (95%)
  between operations  1.28 us (4%)
    pallas_call x1, Pallas kernels, shards(): pl.pallas_call(functools.partial(body, pairs), out_shape=(out, out), in_s...  27.6 us
    pallas_call x1, Pallas kernels, shards(): pl.pallas_call(store, out_shape=(out, out), in_specs=[vmem, vmem], out_sp...  0.72 us

profile of v4, /device:TPU:1, one launch (start us, length us, event | category | flops | bytes accessed | tf_op | source)
XLA Modules:
  0.0 29.6 jit_solution(15699550674857537998)
XLA Ops:
  1.3 27.6 %shard_map.86 = (f32[1,128,256]{2,1,0:T(8,128)S(1)}, f32[1,128,256]{2,1,0:T(8,128)S(1)}) custom-call(bf16[1,256,256]{2,1,0:T(8,128)(2,1)} %amp_hbm.1, s32[1]{0:T(128)S(6)} %copy.9.ranks_hbm, s32[1,8]{1,0:T(1,128)} %nbr_hbm.1, bf16[1,8,256,256]{3,2,1,0:T(8,128)(2,1)} %inter_hbm.1, f32[1,8]{1,0:T(1,128)} %coup_hbm.1, f32[1,256]{1,0:T(1,128)} %energy_hbm.1, ...), custom_call_target="tpu_custom_call" | custom-call | tf_op jit(solution)/shard_map/pallas_call | solution.py:321
  28.9 0.7 %shard_map.87 = (f32[1,128,256]{2,1,0:T(8,128)}, f32[1,128,256]{2,1,0:T(8,128)}) custom-call(f32[1,128,256]{2,1,0:T(8,128)S(1)} %get-tuple-element.4.res_ref, f32[1,128,256]{2,1,0:T(8,128)S(1)} %get-tuple-element.5.upd_ref), custom_call_target="tpu_custom_call" | custom-call | tf_op jit(solution)/shard_map/pallas_call | solution.py:352

commit v5 on v4

v5 whole, which is shorter than its diff:
```python
import functools

import jax
import jax.numpy as jnp
from jax import lax
from jax.experimental import pallas as pl
from jax.experimental.pallas import tpu as pltpu
from jax.sharding import PartitionSpec as P

WIN = 8
RING = 4
REACH = WIN // RING
PIECES = 2
MESH = pl.DeviceIdType.MESH


def body(
    pairs,
    amp_hbm,
    ranks_smem,
    nbr_hbm,
    inter_hbm,
    coup_hbm,
    energy_hbm,
    fact_hbm,
    res_ref,
    upd_ref,
    tbuf,
    sbuf,
    fbuf,
    acc,
    send_half,
    recv_half,
    own_rows,
    energy,
    nbr_s,
    coup_s,
    loc_sem,
    s_send,
    s_recv,
    t_send,
    t_recv,
    r_sem,
    hello,
):
    width = amp_hbm.shape[1]
    half_w = width // 2
    slots = nbr_hbm.shape[1]
    rows_all = pairs // RING
    p = lax.axis_index("pair")
    c = lax.axis_index("aux")
    other = 1 - c
    sibling = (p, other)
    x = lax.rem(p, RING)
    row = p // RING
    cols = pl.ds(pl.multiple_of(c * half_w, half_w), half_w)

    def column(dx):
        return lax.rem(x + dx + RING, RING)

    def far_row(dy):
        return lax.rem(row + dy + rows_all, rows_all)

    def chip(dx, dy):
        return (far_row(dy) * RING + column(dx), c)

    def local(src, dst, k):
        return pltpu.make_async_copy(src, dst, loc_sem.at[k])

    own_tile = tbuf.at[REACH, x]
    loads = [
        local(amp_hbm.at[0, :, cols], own_tile, 1),
        local(energy_hbm, energy, 0),
        local(nbr_hbm.at[0], nbr_s.at[c], 2),
        local(coup_hbm.at[0], coup_s.at[c], 3),
        local(fact_hbm.at[0], fbuf, 4),
        local(inter_hbm.at[0], sbuf.at[pl.ds(c * slots, slots)], 5),
        local(amp_hbm.at[0, cols, :], own_rows, 6),
    ]
    loads[0].start()

    barrier = pltpu.get_barrier_semaphore()
    even = lax.rem(row, 2) == 0

    def greet(sem, peer):
        pl.semaphore_signal(sem, inc=1, device_id=peer, device_id_type=MESH)

    pl.when(even)(lambda: greet(barrier, chip(0, -2)))
    callers = [chip(dx, 0) for dx in (2, 1, 3)] + [chip(0, -1), sibling]
    for peer in callers:
        greet(barrier, peer)
    for copy in loads[1:]:
        copy.start()

    loads[0].wait()
    rank = ranks_smem[0]
    row_id = lax.broadcasted_iota(jnp.int32, (width, half_w), 0)
    col_id = lax.broadcasted_iota(jnp.int32, (width, half_w), 1) + c * half_w
    own_tile[...] = jnp.where(
        (row_id < rank) & (col_id < rank), own_tile[...].astype(jnp.float32), 0.0
    ).astype(jnp.bfloat16)

    pl.semaphore_wait(barrier, len(callers) + jnp.where(even, 1, 0))

    def piece(r, xs, h):
        return tbuf.at[r, xs, pl.ds(h * (width // PIECES), width // PIECES)]

    def send(r, xs, home, k, peer):
        def copy(src, dst, recv_sem):
            return pltpu.make_async_remote_copy(
                src_ref=src, dst_ref=dst, send_sem=t_send.at[k], recv_sem=recv_sem,
                device_id=peer, device_id_type=MESH,
            )

        parts = [
            copy(piece(r, xs, h), piece(home, xs, h), t_recv.at[home, xs, h]) for h in range(PIECES)
        ]
        return parts, copy(tbuf.at[r, xs], tbuf.at[home, xs], t_recv.at[home, xs, 0])

    def start(copies):
        for copy in copies[0]:
            copy.start()

    def sent(group):
        for _, whole in group:
            whole.wait_send()

    top = rows_all - 1
    across = column(2)
    up = [send(REACH, x, REACH - dy, dy - 1, chip(0, dy)) for dy in (1, 2)]
    down = [send(REACH, x, REACH + dy, 1 + dy, chip(0, -dy)) for dy in (1, 2)]
    side = [send(REACH, x, REACH, 3 + dx, chip(dx, 0)) for dx in (2, 1, 3)]
    pass_up = send(REACH, across, REACH - 1, 7, chip(0, 1))
    pass_down = send(REACH, across, REACH + 1, 8, chip(0, -1))
    hand_up = send(REACH - 1, x, REACH - 2, 9, chip(0, 1))
    hand_down = send(REACH + 1, x, REACH + 2, 10, chip(0, -1))
    hand_two = send(REACH - 1, across, 0, 27, chip(0, 1))
    hands_two = (row == 0) & (across > x)
    always = up[:1] + side + down[:1] + [pass_up, pass_down]
    if_even = [up[1], down[1], hand_up, hand_down]
    pl.when(even)(lambda: start(up[1]))
    start(up[0])
    greet(hello.at[0], chip(0, 1))
    pl.when(even)(lambda: greet(hello.at[1], chip(0, 2)))
    for copies in side:
        start(copies)

    def send_down(dy):
        def act():
            pl.semaphore_wait(hello.at[dy - 1], 1)
            start(down[dy - 1])

        if dy == 2:
            pl.when(even)(act)
        else:
            act()

    shares = []
    for k, (src, dst) in enumerate(
        (
            (nbr_hbm.at[0], nbr_s.at[c]),
            (coup_hbm.at[0], coup_s.at[c]),
            (inter_hbm.at[0], sbuf.at[pl.ds(c * slots, slots)]),
        )
    ):
        shares.append(
            pltpu.make_async_remote_copy(
                src_ref=src, dst_ref=dst, send_sem=s_send.at[k], recv_sem=s_recv.at[k],
                device_id=sibling, device_id_type=MESH,
            )
        )
    for copy in shares:
        copy.start()

    for copy in loads[1:]:
        copy.wait()
    acc[...] = lax.dot_general(
        fbuf[0], fbuf[1], (((0,), (0,)), ((), ())), preferred_element_type=jnp.float32
    )

    side_of = jnp.where(row < REACH, 1, -1)

    def late(dy):
        low = (row < dy) & ((row > 0) | (c == 1))
        return low | (top - row < dy)

    def soon(dy):
        return jnp.logical_not(late(dy))

    for dy in (1, 2):
        pl.when(jnp.logical_not(row < dy))(functools.partial(send_down, dy))
    def arrived(r, xs, pieces=range(PIECES)):
        for h in pieces:
            part = piece(r, xs, h)
            pltpu.make_async_copy(part, part, t_recv.at[r, xs, h]).wait()

    def wanted(r, source, dest):
        return ((r > 0) | (dest <= source)) & ((r < 2 * REACH) | (dest >= source))

    def relay_copies(r):
        outer = ((r == 0) & (row != 1)) | (r == 2 * REACH)
        copies = []
        for k, dx in enumerate((2, 1, 3)):
            needed = wanted(r, x, column(dx))
            if dx == 2:
                needed &= outer
            copies.append((needed, send(r, x, r, 11 + 3 * r + k, chip(dx, 0))))
        return copies

    def relay(r):
        copies = relay_copies(r)
        for h in range(PIECES):
            arrived(r, x, (h,))
            pl.when(even & (r == REACH - 1))(hand_up[0][h].start)
            pl.when(even & (r == REACH + 1) & (row > 0))(hand_down[0][h].start)
            for needed, parts in copies:
                pl.when(needed)(parts[0][h].start)

    def entry_of(r, xs):
        q = far_row(r - REACH) * RING + xs
        core, at = jnp.int32(0), jnp.int32(0)
        for k in range(2):
            for n in range(slots):
                hit = nbr_s[k, n] == q
                core, at = jnp.where(hit, k, core), jnp.where(hit, n, at)
        return core * slots + at, jnp.where(nbr_s[core, at] == q, coup_s[core, at], 0.0)

    def picks_of(r):
        found = []
        for dx in (0, 1, 3, 2):
            xs = column(dx)
            needed = wanted(r, xs, x)
            slot, factor = entry_of(r, xs)
            found.append((jnp.where(needed, xs, x), slot, jnp.where(needed, factor, 0.0)))
        for dx in (1, 3, 2):
            xs = column(dx)
            due = wanted(r, xs, x)
            if dx == 2:
                due &= (r != REACH) & ((r != REACH - 1) | (row > 0))
            pl.when(due)(functools.partial(arrived, r, xs))
        return found

    def add_products(r, picks, span):
        total = acc[span, :]
        for xs, slot, factor in picks:
            half = jnp.dot(
                sbuf[slot, span, :], tbuf[r, xs], preferred_element_type=jnp.float32
            ).astype(jnp.bfloat16)
            total += factor * lax.dot_general(
                half, sbuf[slot, :, cols], (((1,), (1,)), ((), ())), preferred_element_type=jnp.float32
            )
        acc[span, :] = total

    def couple_row(r):
        add_products(r, picks_of(r), pl.ds(0, width))

    for h in range(PIECES):
        arrived(REACH, across, (h,))
        pass_up[0][h].start()
        pl.when(row > 0)(pass_down[0][h].start)
    for dy in (1, 2):
        relay(REACH + dy * side_of)

    def other_side(dy):
        def release():
            send_down(dy)
            if dy == 1:
                start(pass_down)
                start(hand_down)

        pl.when(row < dy)(release)
        relay(REACH - dy * side_of)

    for dy in (1, 2):
        pl.when(soon(dy))(functools.partial(other_side, dy))

    for copy in shares:
        copy.wait()

    @pl.loop(0, REACH + 1)
    def _(k):
        couple_row(REACH + k * side_of)

    for dy in (1, 2):
        pl.when(late(dy))(functools.partial(other_side, dy))

    @pl.when(row == 0)
    def _():
        for h in range(PIECES):
            arrived(REACH - 1, across, (h,))
            pl.when(hands_two)(hand_two[0][h].start)

    @pl.loop(1, REACH)
    def _(k):
        couple_row(REACH - k * side_of)

    theirs = pl.ds(pl.multiple_of(other * half_w, half_w), half_w)
    last = REACH - REACH * side_of
    picks = picks_of(last)
    add_products(last, picks, theirs)
    send_half[...] = acc[theirs, :]
    ship = pltpu.make_async_remote_copy(
        src_ref=send_half, dst_ref=recv_half, send_sem=r_sem.at[0], recv_sem=r_sem.at[1],
        device_id=sibling, device_id_type=MESH,
    )
    ship.start()
    add_products(last, picks, cols)
    rows = lax.broadcasted_iota(jnp.int32, (half_w, width), 0) + c * half_w
    columns = lax.broadcasted_iota(jnp.int32, (half_w, width), 1)
    live = (rows < rank) & (columns < rank)
    by_row = jnp.transpose(jnp.broadcast_to(energy[:, cols], (half_w, half_w)))
    denominator = jnp.concatenate([by_row, by_row], axis=1) + energy[...]
    own = jnp.where(live, own_rows[...].astype(jnp.float32), 0.0)
    sent(always)
    pl.when(even)(lambda: sent(if_even))
    pl.when(hands_two)(lambda: sent([hand_two]))

    @pl.loop(0, 2 * REACH + 1)
    def _(r):
        for needed, copies in relay_copies(r):
            pl.when(needed & (r != REACH))(functools.partial(sent, [copies]))

    here = acc[cols, :] + denominator * own
    ship.wait()
    residual = jnp.where(live, here + recv_half[...], 0.0)
    res_ref[0] = residual
    upd_ref[0] = own - residual / denominator


def store(res_ref, upd_ref, res_hbm, upd_hbm, sem):
    copies = [
        pltpu.make_async_copy(src, dst, sem.at[k])
        for k, (src, dst) in enumerate(((res_ref, res_hbm), (upd_ref, upd_hbm)))
    ]
    for copy in copies:
        copy.start()
    for copy in copies:
        copy.wait()


def shards(amplitudes, ranks, neighbours, intersections, couplings, energies, factors):
    pairs = lax.axis_size("pair")
    width = amplitudes.shape[1]
    half_w = width // 2
    slots = neighbours.shape[1]
    span = factors.shape[2]
    out = jax.ShapeDtypeStruct((1, half_w, width), jnp.float32)
    hbm = pl.BlockSpec(memory_space=pltpu.HBM)
    vmem = pl.BlockSpec(memory_space=pltpu.VMEM)
    dma = pltpu.SemaphoreType.DMA
    tiles = (2 * REACH + 1, RING)
    operands = [
        operand if operand.ndim == 1 else pltpu.with_memory_space_constraint(operand, pltpu.HBM)
        for operand in (amplitudes, ranks, neighbours, intersections, couplings, energies, factors)
    ]
    results = pl.pallas_call(
        functools.partial(body, pairs),
        out_shape=(out, out),
        in_specs=[hbm, pl.BlockSpec(memory_space=pltpu.SMEM)] + [hbm] * 5,
        out_specs=(vmem, vmem),
        scratch_shapes=[
            pltpu.VMEM(tiles + (width, half_w), jnp.bfloat16),
            pltpu.VMEM((2 * slots, width, width), jnp.bfloat16),
            pltpu.VMEM((2, span, width), jnp.bfloat16),
            pltpu.VMEM((width, width), jnp.float32),
            pltpu.VMEM((half_w, width), jnp.float32),
            pltpu.VMEM((half_w, width), jnp.float32),
            pltpu.VMEM((half_w, width), jnp.bfloat16),
            pltpu.VMEM((1, width), jnp.float32),
            pltpu.SMEM((2, slots), jnp.int32),
            pltpu.SMEM((2, slots), jnp.float32),
            dma((7,)),
            dma((3,)),
            dma((3,)),
            dma((13 + 3 * (2 * REACH + 1),)),
            dma(tiles + (PIECES,)),
            dma((2,)),
            pltpu.SemaphoreType.REGULAR((2,)),
        ],
        compiler_params=pltpu.CompilerParams(
            collective_id=0, has_side_effects=True, vmem_limit_bytes=VMEM_LIMIT
        ),
    )(*operands)
    return pl.pallas_call(
        store,
        out_shape=(out, out),
        in_specs=[vmem, vmem],
        out_specs=(hbm, hbm),
        scratch_shapes=[dma((2,))],
        compiler_params=pltpu.CompilerParams(vmem_limit_bytes=1 << 20),
    )(*results)


VMEM_LIMIT = 12000000


def solution(mesh):
    return jax.shard_map(
        shards,
        mesh=mesh,
        in_specs=(
            P("pair", None, None),
            P("pair"),
            P("pair", "aux"),
            P("pair", "aux", None, None),
            P("pair", "aux"),
            P("pair", None),
            P("pair", None, "aux", None),
        ),
        out_specs=(P("pair", "aux", None), P("pair", "aux", None)),
        check_vma=False,
    )
```

time: 29.8 us -> 28.8 us (0.966)
  Pallas kernels: 28.3 us -> 27.2 us
    pallas_call x1, Pallas kernels: 27.6 us -> 26.5 us  [shards(): pl.pallas_call(functools.partial(body, pairs), out_shape=(out, out), in_s...]
where the time goes in v5:
time: 28.8 us; the launch traced here: 28.5 us
  Pallas kernels  27.2 us (94%)
  between operations  1.28 us (4%)
    pallas_call x1, Pallas kernels, shards(): pl.pallas_call(functools.partial(body, pairs), out_shape=(out, out), in_s...  26.5 us
    pallas_call x1, Pallas kernels, shards(): pl.pallas_call(store, out_shape=(out, out), in_specs=[vmem, vmem], out_sp...  0.72 us

profile of v5, /device:TPU:1, one launch (start us, length us, event | category | flops | bytes accessed | tf_op | source)
XLA Modules:
  0.0 28.5 jit_solution(12685285280122601886)
XLA Ops:
  1.3 26.5 %shard_map.86 = (f32[1,128,256]{2,1,0:T(8,128)S(1)}, f32[1,128,256]{2,1,0:T(8,128)S(1)}) custom-call(bf16[1,256,256]{2,1,0:T(8,128)(2,1)} %amp_hbm.1, s32[1]{0:T(128)S(6)} %copy.9.ranks_smem, s32[1,8]{1,0:T(1,128)} %nbr_hbm.1, bf16[1,8,256,256]{3,2,1,0:T(8,128)(2,1)} %inter_hbm.1, f32[1,8]{1,0:T(1,128)} %coup_hbm.1, f32[1,256]{1,0:T(1,128)} %energy_hbm.1, ...), custom_call_target="tpu_custom_call" | custom-call | tf_op jit(solution)/shard_map/pallas_call | solution.py:356
  27.8 0.7 %shard_map.87 = (f32[1,128,256]{2,1,0:T(8,128)}, f32[1,128,256]{2,1,0:T(8,128)}) custom-call(f32[1,128,256]{2,1,0:T(8,128)S(1)} %get-tuple-element.4.res_ref, f32[1,128,256]{2,1,0:T(8,128)S(1)} %get-tuple-element.5.upd_ref), custom_call_target="tpu_custom_call" | custom-call | tf_op jit(solution)/shard_map/pallas_call | solution.py:384

commit v6 on v5

--- a/solution.py
+++ b/solution.py
@@ -249,10 +249,10 @@
             total += factor * lax.dot_general(
                 half, sbuf[slot, :, cols], (((1,), (1,)), ((), ())), preferred_element_type=jnp.float32
             )
-        acc[span, :] = total
+        return total
 
     def couple_row(r):
-        add_products(r, picks_of(r), pl.ds(0, width))
+        acc[...] = add_products(r, picks_of(r), pl.ds(0, width))
 
     for h in range(PIECES):
         arrived(REACH, across, (h,))
@@ -277,18 +277,20 @@
     for copy in shares:
         copy.wait()
 
+    def hand_across():
+        for h in range(PIECES):
+            arrived(REACH - 1, across, (h,))
+            pl.when(hands_two)(hand_two[0][h].start)
+
     @pl.loop(0, REACH + 1)
     def _(k):
         couple_row(REACH + k * side_of)
+        pl.when((row == 0) & (c == 0) & (k == 1))(hand_across)
 
     for dy in (1, 2):
         pl.when(late(dy))(functools.partial(other_side, dy))
 
-    @pl.when(row == 0)
-    def _():
-        for h in range(PIECES):
-            arrived(REACH - 1, across, (h,))
-            pl.when(hands_two)(hand_two[0][h].start)
+    pl.when((row == 0) & (c == 1))(hand_across)
 
     @pl.loop(1, REACH)
     def _(k):
@@ -297,14 +299,13 @@
     theirs = pl.ds(pl.multiple_of(other * half_w, half_w), half_w)
     last = REACH - REACH * side_of
     picks = picks_of(last)
-    add_products(last, picks, theirs)
-    send_half[...] = acc[theirs, :]
+    send_half[...] = add_products(last, picks, theirs)
     ship = pltpu.make_async_remote_copy(
         src_ref=send_half, dst_ref=recv_half, send_sem=r_sem.at[0], recv_sem=r_sem.at[1],
         device_id=sibling, device_id_type=MESH,
     )
     ship.start()
-    add_products(last, picks, cols)
+    mine = add_products(last, picks, cols)
     rows = lax.broadcasted_iota(jnp.int32, (half_w, width), 0) + c * half_w
     columns = lax.broadcasted_iota(jnp.int32, (half_w, width), 1)
     live = (rows < rank) & (columns < rank)
@@ -320,7 +321,7 @@
         for needed, copies in relay_copies(r):
             pl.when(needed & (r != REACH))(functools.partial(sent, [copies]))
 
-    here = acc[cols, :] + denominator * own
+    here = mine + denominator * own
     ship.wait()
     residual = jnp.where(live, here + recv_half[...], 0.0)
     res_ref[0] = residual

time: 28.8 us -> 28.8 us (level)
  no operation moved by 1% of the time
where the time goes in v6:
time: 28.8 us; the launch traced here: 28.5 us
  Pallas kernels  27.2 us (94%)
  between operations  1.28 us (4%)
    pallas_call x1, Pallas kernels, shards(): pl.pallas_call(functools.partial(body, pairs), out_shape=(out, out), in_s...  26.5 us
    pallas_call x1, Pallas kernels, shards(): pl.pallas_call(store, out_shape=(out, out), in_specs=[vmem, vmem], out_sp...  0.72 us

profile of v6, /device:TPU:1, one launch (start us, length us, event | category | flops | bytes accessed | tf_op | source)
XLA Modules:
  0.0 28.5 jit_solution(10856699989625233247)
XLA Ops:
  1.3 26.5 %shard_map.86 = (f32[1,128,256]{2,1,0:T(8,128)S(1)}, f32[1,128,256]{2,1,0:T(8,128)S(1)}) custom-call(bf16[1,256,256]{2,1,0:T(8,128)(2,1)} %amp_hbm.1, s32[1]{0:T(128)S(6)} %copy.9.ranks_smem, s32[1,8]{1,0:T(1,128)} %nbr_hbm.1, bf16[1,8,256,256]{3,2,1,0:T(8,128)(2,1)} %inter_hbm.1, f32[1,8]{1,0:T(1,128)} %coup_hbm.1, f32[1,256]{1,0:T(1,128)} %energy_hbm.1, ...), custom_call_target="tpu_custom_call" | custom-call | tf_op jit(solution)/shard_map/pallas_call | solution.py:357
  27.8 0.7 %shard_map.87 = (f32[1,128,256]{2,1,0:T(8,128)}, f32[1,128,256]{2,1,0:T(8,128)}) custom-call(f32[1,128,256]{2,1,0:T(8,128)S(1)} %get-tuple-element.4.res_ref, f32[1,128,256]{2,1,0:T(8,128)S(1)} %get-tuple-element.5.upd_ref), custom_call_target="tpu_custom_call" | custom-call | tf_op jit(solution)/shard_map/pallas_call | solution.py:385

commit v7 on v6

--- a/solution.py
+++ b/solution.py
@@ -134,7 +134,7 @@
     pass_down = send(REACH, across, REACH + 1, 8, chip(0, -1))
     hand_up = send(REACH - 1, x, REACH - 2, 9, chip(0, 1))
     hand_down = send(REACH + 1, x, REACH + 2, 10, chip(0, -1))
-    hand_two = send(REACH - 1, across, 0, 27, chip(0, 1))
+    hand_two = send(REACH - 1, across, 0, 23, chip(0, 1))
     hands_two = (row == 0) & (across > x)
     always = up[:1] + side + down[:1] + [pass_up, pass_down]
     if_even = [up[1], down[1], hand_up, hand_down]
@@ -204,7 +204,7 @@
             needed = wanted(r, x, column(dx))
             if dx == 2:
                 needed &= outer
-            copies.append((needed, send(r, x, r, 11 + 3 * r + k, chip(dx, 0))))
+            copies.append((needed, send(r, x, r, 11 + 3 * (r - jnp.where(r > REACH, 1, 0)) + k, chip(dx, 0))))
         return copies
 
     def relay(r):
@@ -373,7 +373,7 @@
             dma((7,)),
             dma((3,)),
             dma((3,)),
-            dma((13 + 3 * (2 * REACH + 1),)),
+            dma((12 + 3 * 2 * REACH,)),
             dma(tiles + (PIECES,)),
             dma((2,)),
             pltpu.SemaphoreType.REGULAR((2,)),

time: 28.8 us -> 28.8 us (level)
  no operation moved by 1% of the time
where the time goes in v7:
time: 28.8 us; the launch traced here: 28.5 us
  Pallas kernels  27.2 us (94%)
  between operations  1.28 us (4%)
    pallas_call x1, Pallas kernels, shards(): pl.pallas_call(functools.partial(body, pairs), out_shape=(out, out), in_s...  26.5 us
    pallas_call x1, Pallas kernels, shards(): pl.pallas_call(store, out_shape=(out, out), in_specs=[vmem, vmem], out_sp...  0.72 us

profile of v7, /device:TPU:1, one launch (start us, length us, event | category | flops | bytes accessed | tf_op | source)
XLA Modules:
  0.0 28.5 jit_solution(11890921529724458181)
XLA Ops:
  1.3 26.5 %shard_map.86 = (f32[1,128,256]{2,1,0:T(8,128)S(1)}, f32[1,128,256]{2,1,0:T(8,128)S(1)}) custom-call(bf16[1,256,256]{2,1,0:T(8,128)(2,1)} %amp_hbm.1, s32[1]{0:T(128)S(6)} %copy.9.ranks_smem, s32[1,8]{1,0:T(1,128)} %nbr_hbm.1, bf16[1,8,256,256]{3,2,1,0:T(8,128)(2,1)} %inter_hbm.1, f32[1,8]{1,0:T(1,128)} %coup_hbm.1, f32[1,256]{1,0:T(1,128)} %energy_hbm.1, ...), custom_call_target="tpu_custom_call" | custom-call | tf_op jit(solution)/shard_map/pallas_call | solution.py:357
  27.8 0.7 %shard_map.87 = (f32[1,128,256]{2,1,0:T(8,128)}, f32[1,128,256]{2,1,0:T(8,128)}) custom-call(f32[1,128,256]{2,1,0:T(8,128)S(1)} %get-tuple-element.4.res_ref, f32[1,128,256]{2,1,0:T(8,128)S(1)} %get-tuple-element.5.upd_ref), custom_call_target="tpu_custom_call" | custom-call | tf_op jit(solution)/shard_map/pallas_call | solution.py:385
